TPU v7x, 256 devices: a whole 4x4x8 slice. The times are simulated.
256 devices in a mesh: comp: 2 (over y_hi), tile: 128 (over y_lo, x, z, core).
Axes of the slice: x: 4, y: 4 (y_hi: 2, y_lo: 2; y = y_hi * 2 + y_lo), z: 8, core: 2. Of those that a mesh axis runs over, the one named last changes fastest.
Arguments:
- air_winds_heights: float32 [3, 16, 2048, 2048], P(None, None, 'tile', 'comp'), may hold values from -6 to 6
- exchange_coefficient_air: float32 [2048, 2048], P('tile', 'comp'), may hold values from 0.5 to 2
- air_seen_warmness: float32 [2048, 2048], P('tile', 'comp'), may hold values from 1 to 3
- marine_flow_vectors: float32 [2, 10, 1024, 1024], P(None, None, 'tile', 'comp'), may hold values from -6 to 6
- marine_warmness: float32 [1024, 1024], P('tile', 'comp'), may hold values from -6 to 6
- water_indicator: int32 [1024, 1024], P('tile', 'comp'), may hold values 0 or 1
- partner_air_tiles: int32 [8192, 4], P(('comp', 'tile')), may hold values from 0 to 16383, as said below
- partner_tally_each_tile: int32 [8192], P(('comp', 'tile')), may hold values from 2 to 4, as said below
- partner_overlay_shares: bfloat16 [8192, 4, 128, 128], P(('comp', 'tile')), may hold values from 0.0009994507 to 1
Outputs:
- atmosphere_next: float32 [3, 16, 2048, 2048], P(None, None, 'tile', 'comp')
- advanced_flows: float32 [2, 10, 1024, 1024], P(None, None, 'tile', 'comp')
- advanced_warmness: float32 [1024, 1024], P('tile', 'comp')
Inputs may be any that keep to these rules, and one draw needn't show every extreme that they name: `partner_air_tiles`: every entry names an atmosphere block of the ocean block's own longitude half; for ocean block g with t = (g // 32) % 128 it lies from t * 128 - 8 to (t + 1) * 128 + 7, cut to the grid's blocks, and both ends of that range are named for every tile. `partner_tally_each_tile`: the first ocean block of every tile has all 4 slots live.
All inputs are finite; a program needn't handle non-finite values. No bound on the sum of `water_indicator` on one device may be relied on, other than what follows from the above.
Results may differ from a plain program's by a relative error of at most 0.0003.
Values sent between devices are 32-bit elements; how exact they have to be, the bound alone decides.
No kernel may reach another device: no remote copies, remote signals or barrier semaphores. Data moves between devices by JAX's collectives and lax.ppermute only.
A program may use at most 128 MiB of HBM per device.

v0:
```python
import jax
import jax.numpy as jnp
from jax import lax
from jax.sharding import PartitionSpec as P

BLOCK = 128


step_atmos = 0.2
coriolis_atmos = 0.3
visc_atmos = 1.0
mixing_atmos = 0.5
gust_square = 0.25
step_ocean = 0.2
coriolis_ocean = 0.3
visc_ocean = 1.0
mixing_ocean = 0.5
heat_gain = 1.0
diffuse_ocean = 0.5


def extended_2(block, sides, width):
    for axis, dim in sides:
        count = lax.axis_size(axis)
        forward = [(i, i + 1) for i in range(count - 1)]
        backward = [(target, source) for source, target in forward]
        low = lax.ppermute(
            lax.slice_in_dim(block, block.shape[dim] - width, None, axis=dim), axis, forward
        )
        high = lax.ppermute(lax.slice_in_dim(block, 0, width, axis=dim), axis, backward)
        block = jnp.concatenate([low, block, high], axis=dim)
    return block


def vertical(joined_quantities):
    upper = jnp.concatenate([joined_quantities[1:], joined_quantities[-1:]], axis=0)
    lower = jnp.concatenate([joined_quantities[:1], joined_quantities[:-1]], axis=0)
    return upper - 2.0 * joined_quantities + lower


def stencil(bordered_argument):
    centre = bordered_argument[..., 1:-1, 1:-1]
    below_row = bordered_argument[..., :-2, 1:-1]
    above_row = bordered_argument[..., 2:, 1:-1]
    left_col = bordered_argument[..., 1:-1, :-2]
    right_col = bordered_argument[..., 1:-1, 2:]
    laplace = above_row + below_row + left_col + right_col - 4.0 * centre
    east_grad = 0.5 * (right_col - left_col)
    north_grad = 0.5 * (above_row - below_row)
    return (centre, laplace, east_grad, north_grad)


def advance(bordered_argument):
    centre, laplace, east_grad, north_grad = stencil(bordered_argument)
    zonal_flow, meridional_flow, depth_anomaly_sheet = (centre[0], centre[1], centre[2])
    new_east = zonal_flow + step_atmos * (
        coriolis_atmos * meridional_flow
        - east_grad[2]
        + visc_atmos * laplace[0]
        + mixing_atmos * vertical(zonal_flow)
    )
    new_north = meridional_flow + step_atmos * (
        -coriolis_atmos * zonal_flow
        - north_grad[2]
        + visc_atmos * laplace[1]
        + mixing_atmos * vertical(meridional_flow)
    )
    new_thick = depth_anomaly_sheet + step_atmos * (
        -(east_grad[0] + north_grad[1])
        + visc_atmos * laplace[2]
        + mixing_atmos * vertical(depth_anomaly_sheet)
    )
    return jnp.stack([new_east, new_north, new_thick])


def uppermost_sheet(joined_quantities, exchange_coefficient_air, air_seen_warmness):
    zonal_flow = joined_quantities[0, 0]
    meridional_flow = joined_quantities[1, 0]
    depth_anomaly_sheet = joined_quantities[2, 0]
    wind_speed = jnp.sqrt(zonal_flow * zonal_flow + meridional_flow * meridional_flow + gust_square)
    multiplier_coefficient = exchange_coefficient_air * wind_speed
    return jnp.stack(
        [
            multiplier_coefficient * zonal_flow,
            multiplier_coefficient * meridional_flow,
            multiplier_coefficient * (air_seen_warmness - depth_anomaly_sheet),
        ]
    )


def marine_drift_advance(bordered_argument, regridded_exchanges, sea_mask):
    centre, laplace, east_grad, north_grad = stencil(bordered_argument)
    levels = (centre.shape[0] - 1) // 2
    zonal_flow = centre[:levels]
    meridional_flow = centre[levels : 2 * levels]
    warmth = centre[2 * levels]
    blank_levels = jnp.zeros_like(zonal_flow[1:])
    push_east = jnp.concatenate([regridded_exchanges[0][None], blank_levels], axis=0)
    push_north = jnp.concatenate([regridded_exchanges[1][None], blank_levels], axis=0)
    new_east = sea_mask * (
        zonal_flow
        + step_ocean
        * (
            coriolis_ocean * meridional_flow
            + visc_ocean * laplace[:levels]
            + mixing_ocean * vertical(zonal_flow)
            + push_east
        )
    )
    new_north = sea_mask * (
        meridional_flow
        + step_ocean
        * (
            -coriolis_ocean * zonal_flow
            + visc_ocean * laplace[levels : 2 * levels]
            + mixing_ocean * vertical(meridional_flow)
            + push_north
        )
    )
    carried = zonal_flow[0] * east_grad[2 * levels] + meridional_flow[0] * north_grad[2 * levels]
    new_warm = warmth + sea_mask * step_ocean * (
        heat_gain * regridded_exchanges[2] - carried + diffuse_ocean * laplace[2 * levels]
    )
    return (jnp.stack([new_east, new_north]), new_warm)


def shards(
    air_winds_heights,
    exchange_coefficient_air,
    air_seen_warmness,
    marine_flow_vectors,
    marine_warmness,
    water_indicator,
    partner_air_tiles,
    partner_tally_each_tile,
    partner_overlay_shares,
):
    row_count = air_winds_heights.shape[2]
    columns = air_winds_heights.shape[3]
    block_count = row_count * columns // BLOCK
    joined_quantities = air_winds_heights
    for repeat in range(2):
        bordered_argument = extended_2(joined_quantities, (("comp", 3), ("tile", 2)), 1)
        joined_quantities = advance(bordered_argument)
    interface_exchanges = uppermost_sheet(
        joined_quantities, exchange_coefficient_air, air_seen_warmness
    )
    blocks = interface_exchanges.reshape(3, block_count, BLOCK)
    extended = extended_2(blocks, (("tile", 1),), block_count)
    slot_rows = partner_air_tiles - lax.axis_index("tile") * block_count + block_count
    live_slots = (
        jnp.arange(partner_overlay_shares.shape[1], dtype=jnp.int32)[None, :]
        < partner_tally_each_tile[:, None]
    ).astype(jnp.float32)
    chosen = jnp.take(extended, slot_rows, axis=1) * live_slots[None, :, :, None]
    upper_part = chosen.astype(jnp.bfloat16)
    lower_part = (chosen - upper_part.astype(jnp.float32)).astype(jnp.bfloat16)
    live_cells = jnp.broadcast_to(live_slots[None, :, :, None], (1,) + chosen.shape[1:]).astype(
        jnp.bfloat16
    )
    operand = jnp.concatenate([upper_part, lower_part, live_cells], axis=0)
    sums = jnp.einsum(
        "fjsa,jsao->fjo", operand, partner_overlay_shares, preferred_element_type=jnp.float32
    )
    numerator = sums[:3] + sums[3:6]
    denominator = sums[6]
    marine_latitude_number = marine_warmness.shape[0]
    marine_longitude_number = marine_warmness.shape[1]
    regridded_exchanges = (numerator / denominator[None]).reshape(
        3, marine_latitude_number, marine_longitude_number
    )
    joined_arrays = jnp.concatenate(
        [
            marine_flow_vectors.reshape(-1, marine_latitude_number, marine_longitude_number),
            marine_warmness[None],
        ],
        axis=0,
    )
    ocean_padded = extended_2(joined_arrays, (("comp", 2), ("tile", 1)), 1)
    advanced_flows, advanced_warmness = marine_drift_advance(
        ocean_padded, regridded_exchanges, water_indicator.astype(jnp.float32)
    )
    return (joined_quantities, advanced_flows, advanced_warmness)


def solution(mesh):
    placed = (
        P(None, None, "tile", "comp"),
        P("tile", "comp"),
        P("tile", "comp"),
        P(None, None, "tile", "comp"),
        P("tile", "comp"),
        P("tile", "comp"),
        P(("comp", "tile"), None),
        P(("comp", "tile")),
        P(("comp", "tile"), None, None, None),
    )
    return jax.shard_map(
        shards,
        mesh=mesh,
        in_specs=placed,
        out_specs=(P(None, None, "tile", "comp"), P(None, None, "tile", "comp"), P("tile", "comp")),
        check_vma=False,
    )
```

profile of v0, /device:TPU:24, one launch (start us, length us, event | category | flops | bytes accessed | tf_op | source)
XLA Modules:
  0.0 167.3 jit_solution(16263340306633890525)
XLA Ops:
  0.6 1.8 %fusion.72 = (f32[21,8,1]{2,1,0:T(8,128)}, f32[21,8,1]{2,1,0:T(8,128)}) fusion(f32[20,8,512]{2,1,0:T(8,128)} %bitcast.188, f32[1,8,512]{2,1,0:T(8,128)} %bitcast.194), kind=kLoop, calls=%fused_computation.161 | loop fusion | flops 336 | bytes 345408 | tf_op jit(solution)/shard_map/concatenate | solution.py:172
  2.4 3.8 %collective-permute-start.9 = (f32[21,8,1]{2,1,0:T(8,128)}, f32[21,8,1]{2,1,0:T(8,128)}, u32[]{:S(2)}, u32[]{:S(2)}) collective-permute-start(f32[21,8,1]{2,1,0:T(8,128)} %get-tuple-element.73), channel_id=1, source_target_pairs={{128,0},{129,1},{130,2},{131,3},{132,4},{133,5},{134,6},{135,7},{1... | collective-permute-start | bytes 2024 | tf_op jit(solution)/shard_map/ppermute | solution.py:30
  6.2 1.3 collective-permute-start.8
  7.5 2.1 %fusion.96 = (f32[3,16,16,1]{3,2,1,0:T(8,128)}, f32[3,16,16,1]{3,2,1,0:T(8,128)}) fusion(f32[3,16,16,1024]{3,2,1,0:T(8,128)} %param.9), kind=kLoop, calls=%fused_computation.226 | loop fusion | bytes 12288 | tf_op jit(solution)/shard_map/slice | solution.py:28
  9.6 1.3 collective-permute-start.1
  10.9 8.2 %collective-permute-start = (f32[3,16,16,1]{3,2,1,0:T(8,128)}, f32[3,16,16,1]{3,2,1,0:T(8,128)}, u32[]{:S(2)}, u32[]{:S(2)}) collective-permute-start(f32[3,16,16,1]{3,2,1,0:T(8,128)} %get-tuple-element.52), channel_id=1, source_target_pairs={{128,0},{129,1},{130,2},{131,3},{132,4},{133,5},{134,6},{135,7},{1... | collective-permute-start | bytes 9224 | tf_op jit(solution)/shard_map/ppermute | solution.py:30
  19.1 1.4 slice_bitcast_fusion.22
  20.5 2.0 %slice_bitcast_fusion.8 = (f32[9,8,512]{2,1,0:T(8,128)}, f32[9,8,512]{2,1,0:T(8,128)}, f32[9,8,512]{2,1,0:T(8,128)}, f32[9,8,512]{2,1,0:T(8,128)}) fusion(f32[2,10,8,512]{3,2,1,0:T(8,128)} %param.12), kind=kLoop, calls=%fused_computation.158 | loop fusion | bytes 1179648 | tf_op jit(solution)/shard_map/slice | solution.py:37
  23.3 4.6 %slice_bitcast_fusion.33 = (f32[15,16,1024]{2,1,0:T(8,128)}, f32[15,16,1024]{2,1,0:T(8,128)}, f32[15,16,1024]{2,1,0:T(8,128)}, f32[15,16,1024]{2,1,0:T(8,128)}, ...) fusion(f32[3,16,16,1024]{3,2,1,0:T(8,128)S(1)} %copy-done), kind=kLoop, calls=%fused_computation.221 | loop fusion | bytes 17694720 | tf_op jit(solution)/shard_map/slice | solution.py:37
  27.9 1.3 fusion.90
  29.2 1.3 compare_and_fusion
  30.5 1.4 copy.15
  31.9 1.3 reshape.151
  33.2 2.0 %pad_maximum_fusion.30 = (f32[21,1,514]{2,1,0:T(1,128)}, f32[21,1,514]{2,1,0:T(1,128)}) fusion(f32[21,8,1]{2,1,0:T(8,128)} %collective-permute-done.9, f32[21,8,1]{2,1,0:T(8,128)} %collective-permute-done.8, f32[1,8,512]{2,1,0:T(8,128)S(1)} %bitcast.195, f32[20,8,512]{2,1,0:T(8,128)S(1)} %bitcast.189), kind=kLoop, calls=%fused_computation.178 | loop fusion | flops 64764 | bytes 431760 | tf_op jit(solution)/shard_map/concatenate | solution.py:31
  35.2 1.9 %collective-permute-start.11 = (f32[21,1,514]{2,1,0:T(1,128)}, f32[21,1,514]{2,1,0:T(1,128)}, u32[]{:S(2)}, u32[]{:S(2)}) collective-permute-start(f32[21,1,514]{2,1,0:T(1,128)} %get-tuple-element.69), channel_id=1, source_target_pairs={{0,1},{1,2},{2,3},{3,4},{4,5},{5,6},{6,7},{7,8},{8,9},{9,10},{10,1... | collective-permute-start | bytes 129536 | tf_op jit(solution)/shard_map/ppermute | solution.py:27
  37.1 7.9 %collective-permute-start.10 = (f32[21,1,514]{2,1,0:T(1,128)}, f32[21,1,514]{2,1,0:T(1,128)}, u32[]{:S(2)}, u32[]{:S(2)}) collective-permute-start(f32[21,1,514]{2,1,0:T(1,128)} %get-tuple-element.70), channel_id=1, source_target_pairs={{1,0},{2,1},{3,2},{4,3},{5,4},{6,5},{7,6},{8,7},{9,8},{10,9},{11,1... | collective-permute-start | bytes 129536 | tf_op jit(solution)/shard_map/ppermute | solution.py:30
  45.0 4.4 %concatenate.172 = f32[3,16,16,1026]{3,2,1,0:T(8,128)} concatenate(f32[3,16,16,1]{3,2,1,0:T(8,128)} %collective-permute-done.1, f32[3,16,16,1024]{3,2,1,0:T(8,128)S(1)} %copy-done, f32[3,16,16,1]{3,2,1,0:T(8,128)} %collective-permute-done), dimensions={3} | concatenate | bytes 6303744 | tf_op jit(solution)/shard_map/concatenate | solution.py:31
  49.4 3.1 %fusion.94 = (f32[3,16,1,1026]{3,2,1,0:T(1,128)}, f32[3,16,1,1026]{3,2,1,0:T(1,128)}) fusion(f32[3,16,16,1026]{3,2,1,0:T(8,128)} %concatenate.172), kind=kLoop, calls=%fused_computation.224 | loop fusion | bytes 787968 | tf_op jit(solution)/shard_map/slice | solution.py:28
  52.5 1.9 %collective-permute-start.3 = (f32[3,16,1,1026]{3,2,1,0:T(1,128)}, f32[3,16,1,1026]{3,2,1,0:T(1,128)}, u32[]{:S(2)}, u32[]{:S(2)}) collective-permute-start(f32[3,16,1,1026]{3,2,1,0:T(1,128)} %get-tuple-element.23), channel_id=1, source_target_pairs={{0,1},{1,2},{2,3},{3,4},{4,5},{5,6},{6,7},{7,8},{8,9},{9,10},{10,1... | collective-permute-start | bytes 590984 | tf_op jit(solution)/shard_map/ppermute | solution.py:27
  54.4 8.0 %collective-permute-start.2 = (f32[3,16,1,1026]{3,2,1,0:T(1,128)}, f32[3,16,1,1026]{3,2,1,0:T(1,128)}, u32[]{:S(2)}, u32[]{:S(2)}) collective-permute-start(f32[3,16,1,1026]{3,2,1,0:T(1,128)} %get-tuple-element.24), channel_id=1, source_target_pairs={{1,0},{2,1},{3,2},{4,3},{5,4},{6,5},{7,6},{8,7},{9,8},{10,9},{11,1... | collective-permute-start | bytes 590984 | tf_op jit(solution)/shard_map/ppermute | solution.py:30
  62.5 1.2 pad_clamp_fusion
  63.7 1.3 copy.14
  65.0 1.3 convert_element_type.23
  66.3 2.6 %pad_maximum_fusion.24 = (f32[21,8,512]{2,1,0:T(8,128)}, f32[21,8,512]{2,1,0:T(8,128)}, f32[21,8,512]{2,1,0:T(8,128)}, f32[21,8,512]{2,1,0:T(8,128)}) fusion(f32[21,1,514]{2,1,0:T(1,128)} %collective-permute-done.10, f32[21,8,1]{2,1,0:T(8,128)} %collective-permute-done.9, f32[21,8,1]{2,1,0:T(8,128)} %collective-permute-done.8, ...), kind=kLoop, calls=%fused_computation.115 | loop fusion | flops 1032192 | bytes 1808016 | tf_op jit(solution)/shard_map/concatenate | solution.py:31
  69.0 7.5 %subtract_multiply_fusion.2 = (f32[3,16,16,1024]{3,2,1,0:T(8,128)S(1)}, f32[3,16,16,1024]{3,2,1,0:T(8,128)S(1)}, f32[3,16,16,1024]{3,2,1,0:T(8,128)S(1)}) fusion(f32[3,16,1,1026]{3,2,1,0:T(1,128)} %collective-permute-done.2, f32[3,16,16,1026]{3,2,1,0:T(8,128)} %concatenate.172, f32[3,16,1,1026]{3,2,1,0:T(1,128)} %collective-permute-done.3, ...), kind=kLoop, calls=%fused_computation.18 | loop fusion | flops 10223616 | bytes 16134912 | tf_op jit(solution)/shard_map/mul | solution.py:49
  76.6 1.7 %fusion.30 = (f32[16,16,1024]{2,1,0:T(8,128)S(1)}, f32[16,16,1024]{2,1,0:T(8,128)S(1)}) fusion(f32[1,16,1024]{2,1,0:T(8,128)S(1)} %copy-done.44, f32[15,16,1024]{2,1,0:T(8,128)S(1)} %copy-done.18, f32[15,16,1024]{2,1,0:T(8,128)S(1)} %copy-done.17, f32[1,16,1024]{2,1,0:T(8,128)S(1)} %copy-done.43, f32[3,16,16,1024]{3,2,1,0:T(8,128)S(1)} %get-tuple-element.19, ...), kind=kLoop, calls=%fused_computation.64 | loop fusion | flops 6291456 | bytes 14680064 | tf_op jit(solution)/shard_map/add | solution.py:56
  79.0 2.1 %slice_bitcast_fusion = (f32[1,15,16,1024]{3,2,1,0:T(8,128)}, f32[1,15,16,1024]{3,2,1,0:T(8,128)}, f32[1,15,16,1024]{3,2,1,0:T(8,128)}, f32[1,15,16,1024]{3,2,1,0:T(8,128)}) fusion(f32[16,16,1024]{2,1,0:T(8,128)S(1)} %get-tuple-element.11, f32[16,16,1024]{2,1,0:T(8,128)S(1)} %get-tuple-element.10), kind=kLoop, calls=%fused_computation.95 | loop fusion | bytes 7864320 | tf_op jit(solution)/shard_map/concatenate | solution.py:37
  82.4 1.5 slice_bitcast_fusion.2
  87.1 1.7 %fusion.15 = (f32[1,16,16,1024]{3,2,1,0:T(8,128)S(1)}, f32[1,16,16,1024]{3,2,1,0:T(8,128)S(1)}) fusion(f32[1,1,16,1024]{3,2,1,0:T(8,128)S(1)} %copy-done.36, f32[1,15,16,1024]{3,2,1,0:T(8,128)S(1)} %copy-done.15, f32[1,15,16,1024]{3,2,1,0:T(8,128)S(1)} %copy-done.14, f32[1,1,16,1024]{3,2,1,0:T(8,128)S(1)} %get-tuple-element.33, ...), kind=kLoop, calls=%fused_computation.46 | loop fusion | flops 6291456 | bytes 14680064 | tf_op jit(solution)/shard_map/add | solution.py:56
  90.3 2.2 %collective-permute-start.4 = (f32[3,16,16,1]{3,2,1,0:T(8,128)S(1)}, f32[3,16,16,1]{3,2,1,0:T(8,128)}, u32[]{:S(2)}, u32[]{:S(2)}) collective-permute-start(f32[3,16,16,1]{3,2,1,0:T(8,128)S(1)} %get-tuple-element.49), channel_id=1, source_target_pairs={{128,0},{129,1},{130,2},{131,3},{132,4},{133,5},{134,6},{135,7},{1... | collective-permute-start | bytes 9224 | tf_op jit(solution)/shard_map/ppermute | solution.py:30
  92.5 1.3 collective-permute-start.5
  94.5 2.6 %collective-permute-done.4 = f32[3,16,16,1]{3,2,1,0:T(8,128)} collective-permute-done((f32[3,16,16,1]{3,2,1,0:T(8,128)S(1)}, f32[3,16,16,1]{3,2,1,0:T(8,128)}, u32[]{:S(2)}, u32[]{:S(2)}) %collective-permute-start.4) | collective-permute-done | bytes 3104 | tf_op jit(solution)/shard_map/ppermute | solution.py:30
  97.0 6.8 %collective-permute-done.5 = f32[3,16,16,1]{3,2,1,0:T(8,128)} collective-permute-done((f32[3,16,16,1]{3,2,1,0:T(8,128)S(1)}, f32[3,16,16,1]{3,2,1,0:T(8,128)}, u32[]{:S(2)}, u32[]{:S(2)}) %collective-permute-start.5) | collective-permute-done | bytes 3104 | tf_op jit(solution)/shard_map/ppermute | solution.py:27
  103.8 4.9 %concatenate.183 = f32[3,16,16,1026]{3,2,1,0:T(8,128)} concatenate(f32[3,16,16,1]{3,2,1,0:T(8,128)} %collective-permute-done.5, f32[3,16,16,1024]{3,2,1,0:T(8,128)} %copy-done.9, f32[3,16,16,1]{3,2,1,0:T(8,128)} %collective-permute-done.4), dimensions={3} | concatenate | bytes 6303744 | tf_op jit(solution)/shard_map/concatenate | solution.py:31
  108.7 2.3 %fusion.93 = (f32[3,16,1,1026]{3,2,1,0:T(1,128)S(1)}, f32[3,16,1,1026]{3,2,1,0:T(1,128)S(1)}) fusion(f32[3,16,16,1026]{3,2,1,0:T(8,128)} %concatenate.183), kind=kLoop, calls=%fused_computation.223 | loop fusion | bytes 787968 | tf_op jit(solution)/shard_map/slice | solution.py:28
  111.0 1.9 %collective-permute-start.7 = (f32[3,16,1,1026]{3,2,1,0:T(1,128)S(1)}, f32[3,16,1,1026]{3,2,1,0:T(1,128)S(1)}, u32[]{:S(2)}, u32[]{:S(2)}) collective-permute-start(f32[3,16,1,1026]{3,2,1,0:T(1,128)S(1)} %get-tuple-element.21), channel_id=1, source_target_pairs={{0,1},{1,2},{2,3},{3,4},{4,5},{5,6},{6,7},{7,8},{8,9},{9,10},{10,1... | collective-permute-start | bytes 590984 | tf_op jit(solution)/shard_map/ppermute | solution.py:27
  112.9 8.3 %collective-permute-start.6 = (f32[3,16,1,1026]{3,2,1,0:T(1,128)S(1)}, f32[3,16,1,1026]{3,2,1,0:T(1,128)S(1)}, u32[]{:S(2)}, u32[]{:S(2)}) collective-permute-start(f32[3,16,1,1026]{3,2,1,0:T(1,128)S(1)} %get-tuple-element.22), channel_id=1, source_target_pairs={{1,0},{2,1},{3,2},{4,3},{5,4},{6,5},{7,6},{8,7},{9,8},{10,9},{11,1... | collective-permute-start | bytes 590984 | tf_op jit(solution)/shard_map/ppermute | solution.py:30
  121.3 4.4 %subtract_multiply_fusion.1 = f32[3,16,16,1024]{3,2,1,0:T(8,128)S(1)} fusion(f32[3,16,16,1]{3,2,1,0:T(8,128)} %collective-permute-done.4, f32[1,16,16,1024]{3,2,1,0:T(8,128)S(1)} %copy-done.6, f32[1,16,16,1024]{3,2,1,0:T(8,128)S(1)} %copy-done.4, f32[1,16,16,1024]{3,2,1,0:T(8,128)S(1)} %copy-done.2, f32[3,16,16,1]{3,2,1,0:T(8,128)} %collective-permute-done.5), kind=kLoop, calls=%fused_computation.17 | loop fusion | flops 6291456 | bytes 6297600 | tf_op jit(solution)/shard_map/mul | solution.py:48
  125.7 7.6 %subtract_multiply_fusion = (f32[3,16,16,1024]{3,2,1,0:T(8,128)S(1)}, f32[3,16,16,1024]{3,2,1,0:T(8,128)S(1)}) fusion(f32[3,16,1,1026]{3,2,1,0:T(1,128)S(1)} %collective-permute-done.6, f32[3,16,16,1026]{3,2,1,0:T(8,128)S(1)} %copy-done.8, f32[3,16,1,1026]{3,2,1,0:T(1,128)S(1)} %collective-permute-done.7, f32[1,16,16,1024]{3,2,1,0:T(8,128)S(1)} %copy-done.6, ...), kind=kLoop, calls=%fused_computation.15 | loop fusion | flops 13369344 | bytes 12989184 | tf_op jit(solution)/shard_map/mul | solution.py:49
  135.9 2.7 %fusion.9 = (f32[1,16,16,1024]{3,2,1,0:T(8,128)S(1)}, f32[1,16,16,1024]{3,2,1,0:T(8,128)}) fusion(f32[1,16,16,1024]{3,2,1,0:T(8,128)S(1)} %copy-done.2, f32[3,16,16,1024]{3,2,1,0:T(8,128)S(1)} %get-tuple-element.17, f32[3,16,16,1024]{3,2,1,0:T(8,128)S(1)} %subtract_multiply_fusion.1, f32[1,1,16,1024]{3,2,1,0:T(8,128)S(1)} %copy-done.50, ...), kind=kLoop, calls=%fused_computation.36 | loop fusion | flops 6291456 | bytes 14680064 | tf_op jit(solution)/shard_map/add | solution.py:56
  138.7 0.9 copy-done.11
  141.0 6.6 %collective-permute-start.13 = (f32[3,128,128]{2,0,1:T(4,128)S(1)}, f32[3,128,128]{2,0,1:T(4,128)S(1)}, u32[]{:S(2)}, u32[]{:S(2)}) collective-permute-start(f32[3,128,128]{2,0,1:T(4,128)S(1)} %pad_maximum_fusion.29), channel_id=1, source_target_pairs={{1,0},{2,1},{3,2},{4,3},{5,4},{6,5},{7,6},{8,7},{9,8},{10,9},{11,1... | collective-permute-start | bytes 589832 | tf_op jit(solution)/shard_map/ppermute | solution.py:30
  147.6 1.9 %collective-permute-start.12 = (f32[3,128,128]{2,0,1:T(4,128)S(1)}, f32[3,128,128]{2,0,1:T(4,128)S(1)}, u32[]{:S(2)}, u32[]{:S(2)}) collective-permute-start(f32[3,128,128]{2,0,1:T(4,128)S(1)} %pad_maximum_fusion.29), channel_id=1, source_target_pairs={{0,1},{1,2},{2,3},{3,4},{4,5},{5,6},{6,7},{7,8},{8,9},{9,10},{10,1... | collective-permute-start | bytes 589832 | tf_op jit(solution)/shard_map/ppermute | solution.py:27
  149.5 1.5 fusion.48
  151.1 3.6 %pad_maximum_fusion.13 = f32[3,16,16,1024]{3,2,1,0:T(8,128)} fusion(f32[1,16,16,1024]{3,2,1,0:T(8,128)S(1)} %copy-done.12, f32[1,16,16,1024]{3,2,1,0:T(8,128)} %copy-done.10, f32[1,16,16,1024]{3,2,1,0:T(8,128)} %copy-done.11), kind=kLoop, calls=%fused_computation.14 | loop fusion | flops 1572864 | bytes 6291456 | tf_op jit(solution)/shard_map/stack | solution.py:73
  154.7 4.8 %collective-permute-done.12 = f32[3,128,128]{2,0,1:T(4,128)S(1)} collective-permute-done((f32[3,128,128]{2,0,1:T(4,128)S(1)}, f32[3,128,128]{2,0,1:T(4,128)S(1)}, u32[]{:S(2)}, u32[]{:S(2)}) %collective-permute-start.12) | collective-permute-done | bytes 196640 | tf_op jit(solution)/shard_map/ppermute | solution.py:27
  161.6 3.0 %convolution_bitcast_fusion = f32[7,32,128]{2,0,1:T(8,128)S(1)} fusion(bf16[32,4,128,128]{3,2,1,0:T(8,128)(2,1)} %param.17, bf16[1,32,4,128]{3,0,2,1:T(2,128)(2,1)S(1)} %broadcast_in_dim.31, bf16[3,32,4,128]{3,0,2,1:T(4,128)(2,1)S(1)} %fusion.54, bf16[3,32,4,128]{3,0,2,1:T(4,128)(2,1)S(1)} %bitcast_convert_fusion), kind=kOutput, calls=%fused_computation.21 | convolution fusion | flops 30048256 | bytes 4538368 | tf_op jit(solution)/shard_map/fjsa,jsao->fjo/dot_general | solution.py:162
  165.9 1.4 fusion.81
  (165 shorter events, 15.0 us)
Async XLA Ops:
  0.6 21.8 %copy-start = (f32[3,16,16,1024]{3,2,1,0:T(8,128)S(1)}, f32[3,16,16,1024]{3,2,1,0:T(8,128)}, u32[]{:S(2)}) copy-start(f32[3,16,16,1024]{3,2,1,0:T(8,128)} %param.9) | copy-start | bytes 9437188
  2.4 30.8 %collective-permute-start.9 = (f32[21,8,1]{2,1,0:T(8,128)}, f32[21,8,1]{2,1,0:T(8,128)}, u32[]{:S(2)}, u32[]{:S(2)}) collective-permute-start(f32[21,8,1]{2,1,0:T(8,128)} %get-tuple-element.73), channel_id=1, source_target_pairs={{128,0},{129,1},{130,2},{131,3},{132,4},{133,5},{134,6},{135,7},{1... | collective-permute-start | bytes 2024 | tf_op jit(solution)/shard_map/ppermute | solution.py:30
  6.2 27.0 %collective-permute-start.8 = (f32[21,8,1]{2,1,0:T(8,128)}, f32[21,8,1]{2,1,0:T(8,128)}, u32[]{:S(2)}, u32[]{:S(2)}) collective-permute-start(f32[21,8,1]{2,1,0:T(8,128)} %get-tuple-element.74), channel_id=1, source_target_pairs={{0,128},{1,129},{2,130},{3,131},{4,132},{5,133},{6,134},{7,135},{8... | collective-permute-start | bytes 2024 | tf_op jit(solution)/shard_map/ppermute | solution.py:27
  9.6 35.4 %collective-permute-start.1 = (f32[3,16,16,1]{3,2,1,0:T(8,128)}, f32[3,16,16,1]{3,2,1,0:T(8,128)}, u32[]{:S(2)}, u32[]{:S(2)}) collective-permute-start(f32[3,16,16,1]{3,2,1,0:T(8,128)} %get-tuple-element.51), channel_id=1, source_target_pairs={{0,128},{1,129},{2,130},{3,131},{4,132},{5,133},{6,134},{7,135},{8... | collective-permute-start | bytes 9224 | tf_op jit(solution)/shard_map/ppermute | solution.py:27
  10.9 34.1 %collective-permute-start = (f32[3,16,16,1]{3,2,1,0:T(8,128)}, f32[3,16,16,1]{3,2,1,0:T(8,128)}, u32[]{:S(2)}, u32[]{:S(2)}) collective-permute-start(f32[3,16,16,1]{3,2,1,0:T(8,128)} %get-tuple-element.52), channel_id=1, source_target_pairs={{128,0},{129,1},{130,2},{131,3},{132,4},{133,5},{134,6},{135,7},{1... | collective-permute-start | bytes 9224 | tf_op jit(solution)/shard_map/ppermute | solution.py:30
  23.3 9.9 %copy-start.7 = (f32[2,10,8,512]{3,2,1,0:T(8,128)S(1)}, f32[2,10,8,512]{3,2,1,0:T(8,128)}, u32[]{:S(2)}) copy-start(f32[2,10,8,512]{3,2,1,0:T(8,128)} %param.12) | copy-start | bytes 983044
  23.3 9.9 %copy-start.35 = (f32[8,512]{1,0:T(8,128)S(1)}, f32[8,512]{1,0:T(8,128)}, u32[]{:S(2)}) copy-start(f32[8,512]{1,0:T(8,128)} %param.13) | copy-start | bytes 49156
  35.2 31.1 %collective-permute-start.11 = (f32[21,1,514]{2,1,0:T(1,128)}, f32[21,1,514]{2,1,0:T(1,128)}, u32[]{:S(2)}, u32[]{:S(2)}) collective-permute-start(f32[21,1,514]{2,1,0:T(1,128)} %get-tuple-element.69), channel_id=1, source_target_pairs={{0,1},{1,2},{2,3},{3,4},{4,5},{5,6},{6,7},{7,8},{8,9},{9,10},{10,1... | collective-permute-start | bytes 129536 | tf_op jit(solution)/shard_map/ppermute | solution.py:27
  37.1 29.2 %collective-permute-start.10 = (f32[21,1,514]{2,1,0:T(1,128)}, f32[21,1,514]{2,1,0:T(1,128)}, u32[]{:S(2)}, u32[]{:S(2)}) collective-permute-start(f32[21,1,514]{2,1,0:T(1,128)} %get-tuple-element.70), channel_id=1, source_target_pairs={{1,0},{2,1},{3,2},{4,3},{5,4},{6,5},{7,6},{8,7},{9,8},{10,9},{11,1... | collective-permute-start | bytes 129536 | tf_op jit(solution)/shard_map/ppermute | solution.py:30
  52.5 16.5 %collective-permute-start.3 = (f32[3,16,1,1026]{3,2,1,0:T(1,128)}, f32[3,16,1,1026]{3,2,1,0:T(1,128)}, u32[]{:S(2)}, u32[]{:S(2)}) collective-permute-start(f32[3,16,1,1026]{3,2,1,0:T(1,128)} %get-tuple-element.23), channel_id=1, source_target_pairs={{0,1},{1,2},{2,3},{3,4},{4,5},{5,6},{6,7},{7,8},{8,9},{9,10},{10,1... | collective-permute-start | bytes 590984 | tf_op jit(solution)/shard_map/ppermute | solution.py:27
  54.4 14.6 %collective-permute-start.2 = (f32[3,16,1,1026]{3,2,1,0:T(1,128)}, f32[3,16,1,1026]{3,2,1,0:T(1,128)}, u32[]{:S(2)}, u32[]{:S(2)}) collective-permute-start(f32[3,16,1,1026]{3,2,1,0:T(1,128)} %get-tuple-element.24), channel_id=1, source_target_pairs={{1,0},{2,1},{3,2},{4,3},{5,4},{6,5},{7,6},{8,7},{9,8},{10,9},{11,1... | collective-permute-start | bytes 590984 | tf_op jit(solution)/shard_map/ppermute | solution.py:30
  68.9 7.5 %copy-start.17 = (f32[15,16,1024]{2,1,0:T(8,128)S(1)}, f32[15,16,1024]{2,1,0:T(8,128)}, u32[]{:S(2)}) copy-start(f32[15,16,1024]{2,1,0:T(8,128)} %get-tuple-element.37) | copy-start | bytes 2949124
  68.9 7.6 %copy-start.18 = (f32[15,16,1024]{2,1,0:T(8,128)S(1)}, f32[15,16,1024]{2,1,0:T(8,128)}, u32[]{:S(2)}) copy-start(f32[15,16,1024]{2,1,0:T(8,128)} %get-tuple-element.38) | copy-start | bytes 2949124
  68.9 7.6 %copy-start.19 = (f32[15,16,1024]{2,1,0:T(8,128)S(1)}, f32[15,16,1024]{2,1,0:T(8,128)}, u32[]{:S(2)}) copy-start(f32[15,16,1024]{2,1,0:T(8,128)} %get-tuple-element.41) | copy-start | bytes 2949124
  68.9 7.6 %copy-start.20 = (f32[15,16,1024]{2,1,0:T(8,128)S(1)}, f32[15,16,1024]{2,1,0:T(8,128)}, u32[]{:S(2)}) copy-start(f32[15,16,1024]{2,1,0:T(8,128)} %get-tuple-element.42) | copy-start | bytes 2949124
  68.9 7.6 %copy-start.43 = (f32[1,16,1024]{2,1,0:T(8,128)S(1)}, f32[1,16,1024]{2,1,0:T(8,128)}, u32[]{:S(2)}) copy-start(f32[1,16,1024]{2,1,0:T(8,128)} %get-tuple-element.25) | copy-start | bytes 196612
  69.0 7.6 %copy-start.44 = (f32[1,16,1024]{2,1,0:T(8,128)S(1)}, f32[1,16,1024]{2,1,0:T(8,128)}, u32[]{:S(2)}) copy-start(f32[1,16,1024]{2,1,0:T(8,128)} %get-tuple-element.26) | copy-start | bytes 196612
  69.0 7.6 %copy-start.45 = (f32[1,16,1024]{2,1,0:T(8,128)S(1)}, f32[1,16,1024]{2,1,0:T(8,128)}, u32[]{:S(2)}) copy-start(f32[1,16,1024]{2,1,0:T(8,128)} %get-tuple-element.29) | copy-start | bytes 196612
  69.0 7.6 %copy-start.46 = (f32[1,16,1024]{2,1,0:T(8,128)S(1)}, f32[1,16,1024]{2,1,0:T(8,128)}, u32[]{:S(2)}) copy-start(f32[1,16,1024]{2,1,0:T(8,128)} %get-tuple-element.30) | copy-start | bytes 196612
  90.3 6.7 %collective-permute-start.4 = (f32[3,16,16,1]{3,2,1,0:T(8,128)S(1)}, f32[3,16,16,1]{3,2,1,0:T(8,128)}, u32[]{:S(2)}, u32[]{:S(2)}) collective-permute-start(f32[3,16,16,1]{3,2,1,0:T(8,128)S(1)} %get-tuple-element.49), channel_id=1, source_target_pairs={{128,0},{129,1},{130,2},{131,3},{132,4},{133,5},{134,6},{135,7},{1... | collective-permute-start | bytes 9224 | tf_op jit(solution)/shard_map/ppermute | solution.py:30
  92.5 11.3 %collective-permute-start.5 = (f32[3,16,16,1]{3,2,1,0:T(8,128)S(1)}, f32[3,16,16,1]{3,2,1,0:T(8,128)}, u32[]{:S(2)}, u32[]{:S(2)}) collective-permute-start(f32[3,16,16,1]{3,2,1,0:T(8,128)S(1)} %get-tuple-element.50), channel_id=1, source_target_pairs={{0,128},{1,129},{2,130},{3,131},{4,132},{5,133},{6,134},{7,135},{8... | collective-permute-start | bytes 9224 | tf_op jit(solution)/shard_map/ppermute | solution.py:27
  94.4 26.8 %copy-start.2 = (f32[1,16,16,1024]{3,2,1,0:T(8,128)S(1)}, f32[1,16,16,1024]{3,2,1,0:T(8,128)}, u32[]{:S(2)}) copy-start(f32[1,16,16,1024]{3,2,1,0:T(8,128)} %copy-done.1) | copy-start | bytes 3145732
  94.4 26.8 %copy-start.4 = (f32[1,16,16,1024]{3,2,1,0:T(8,128)S(1)}, f32[1,16,16,1024]{3,2,1,0:T(8,128)}, u32[]{:S(2)}) copy-start(f32[1,16,16,1024]{3,2,1,0:T(8,128)} %copy-done.3) | copy-start | bytes 3145732
  94.4 26.8 %copy-start.6 = (f32[1,16,16,1024]{3,2,1,0:T(8,128)S(1)}, f32[1,16,16,1024]{3,2,1,0:T(8,128)}, u32[]{:S(2)}) copy-start(f32[1,16,16,1024]{3,2,1,0:T(8,128)} %copy-done.5) | copy-start | bytes 3145732
  111.0 14.8 %collective-permute-start.7 = (f32[3,16,1,1026]{3,2,1,0:T(1,128)S(1)}, f32[3,16,1,1026]{3,2,1,0:T(1,128)S(1)}, u32[]{:S(2)}, u32[]{:S(2)}) collective-permute-start(f32[3,16,1,1026]{3,2,1,0:T(1,128)S(1)} %get-tuple-element.21), channel_id=1, source_target_pairs={{0,1},{1,2},{2,3},{3,4},{4,5},{5,6},{6,7},{7,8},{8,9},{9,10},{10,1... | collective-permute-start | bytes 590984 | tf_op jit(solution)/shard_map/ppermute | solution.py:27
  112.9 12.8 %copy-start.8 = (f32[3,16,16,1026]{3,2,1,0:T(8,128)S(1)}, f32[3,16,16,1026]{3,2,1,0:T(8,128)}, u32[]{:S(2)}) copy-start(f32[3,16,16,1026]{3,2,1,0:T(8,128)} %concatenate.183) | copy-start | bytes 9455620
  112.9 12.8 %collective-permute-start.6 = (f32[3,16,1,1026]{3,2,1,0:T(1,128)S(1)}, f32[3,16,1,1026]{3,2,1,0:T(1,128)S(1)}, u32[]{:S(2)}, u32[]{:S(2)}) collective-permute-start(f32[3,16,1,1026]{3,2,1,0:T(1,128)S(1)} %get-tuple-element.22), channel_id=1, source_target_pairs={{1,0},{2,1},{3,2},{4,3},{5,4},{6,5},{7,6},{8,7},{9,8},{10,9},{11,1... | collective-permute-start | bytes 590984 | tf_op jit(solution)/shard_map/ppermute | solution.py:30
  125.7 7.7 %copy-start.29 = (f32[1,15,16,1024]{3,2,1,0:T(8,128)S(1)}, f32[1,15,16,1024]{3,2,1,0:T(8,128)}, u32[]{:S(2)}) copy-start(f32[1,15,16,1024]{3,2,1,0:T(8,128)} %get-tuple-element.59) | copy-start | bytes 2949124
  125.7 7.7 %copy-start.30 = (f32[1,15,16,1024]{3,2,1,0:T(8,128)S(1)}, f32[1,15,16,1024]{3,2,1,0:T(8,128)}, u32[]{:S(2)}) copy-start(f32[1,15,16,1024]{3,2,1,0:T(8,128)} %get-tuple-element.60) | copy-start | bytes 2949124
  125.7 7.7 %copy-start.47 = (f32[1,1,16,1024]{3,2,1,0:T(8,128)S(1)}, f32[1,1,16,1024]{3,2,1,0:T(8,128)}, u32[]{:S(2)}) copy-start(f32[1,1,16,1024]{3,2,1,0:T(8,128)} %get-tuple-element.58) | copy-start | bytes 196612
  134.2 4.4 %copy-start.10 = (f32[1,16,16,1024]{3,2,1,0:T(8,128)}, f32[1,16,16,1024]{3,2,1,0:T(8,128)S(1)}, u32[]{:S(2)}) copy-start(f32[1,16,16,1024]{3,2,1,0:T(8,128)S(1)} %fusion.6) | copy-start | bytes 3145732
  138.6 12.4 %copy-start.12 = (f32[1,16,16,1024]{3,2,1,0:T(8,128)S(1)}, f32[1,16,16,1024]{3,2,1,0:T(8,128)}, u32[]{:S(2)}) copy-start(f32[1,16,16,1024]{3,2,1,0:T(8,128)} %get-tuple-element.15) | copy-start | bytes 3145732
  141.0 13.8 %collective-permute-start.13 = (f32[3,128,128]{2,0,1:T(4,128)S(1)}, f32[3,128,128]{2,0,1:T(4,128)S(1)}, u32[]{:S(2)}, u32[]{:S(2)}) collective-permute-start(f32[3,128,128]{2,0,1:T(4,128)S(1)} %pad_maximum_fusion.29), channel_id=1, source_target_pairs={{1,0},{2,1},{3,2},{4,3},{5,4},{6,5},{7,6},{8,7},{9,8},{10,9},{11,1... | collective-permute-start | bytes 589832 | tf_op jit(solution)/shard_map/ppermute | solution.py:30
  147.6 11.9 %collective-permute-start.12 = (f32[3,128,128]{2,0,1:T(4,128)S(1)}, f32[3,128,128]{2,0,1:T(4,128)S(1)}, u32[]{:S(2)}, u32[]{:S(2)}) collective-permute-start(f32[3,128,128]{2,0,1:T(4,128)S(1)} %pad_maximum_fusion.29), channel_id=1, source_target_pairs={{0,1},{1,2},{2,3},{3,4},{4,5},{5,6},{6,7},{7,8},{8,9},{9,10},{10,1... | collective-permute-start | bytes 589832 | tf_op jit(solution)/shard_map/ppermute | solution.py:27
  151.1 8.7 %copy-start.53 = (s32[1024]{0:T(1024)S(1)}, s32[1024]{0:T(1024)}, u32[]{:S(2)}) copy-start(s32[1024]{0:T(1024)} %pad_clamp_fusion) | copy-start | bytes 12292
  151.1 9.6 %copy-start.52 = (f32[32,4]{1,0:T(8,128)S(1)}, f32[32,4]{1,0:T(8,128)}, u32[]{:S(2)}) copy-start(f32[32,4]{1,0:T(8,128)} %get-tuple-element.85) | copy-start | bytes 1540
  151.1 9.6 %copy-start.62 = (pred[32,4]{1,0:T(8,128)(4,1)S(1)}, pred[32,4]{1,0:T(8,128)(4,1)}, u32[]{:S(2)}) copy-start(pred[32,4]{1,0:T(8,128)(4,1)} %copy.14) | copy-start | bytes 388
  151.1 10.3 %copy-start.63 = (bf16[32,4]{1,0:T(8,128)(2,1)S(1)}, bf16[32,4]{1,0:T(8,128)(2,1)}, u32[]{:S(2)}) copy-start(bf16[32,4]{1,0:T(8,128)(2,1)} %get-tuple-element.86) | copy-start | bytes 772
  159.8 5.0 %copy-start.31 = (f32[9,8,512]{2,1,0:T(8,128)S(1)}, f32[9,8,512]{2,1,0:T(8,128)}, u32[]{:S(2)}) copy-start(f32[9,8,512]{2,1,0:T(8,128)} %get-tuple-element.79) | copy-start | bytes 442372
  159.8 5.0 %copy-start.32 = (f32[9,8,512]{2,1,0:T(8,128)S(1)}, f32[9,8,512]{2,1,0:T(8,128)}, u32[]{:S(2)}) copy-start(f32[9,8,512]{2,1,0:T(8,128)} %get-tuple-element.80) | copy-start | bytes 442372
  159.8 5.0 %copy-start.33 = (f32[9,8,512]{2,1,0:T(8,128)S(1)}, f32[9,8,512]{2,1,0:T(8,128)}, u32[]{:S(2)}) copy-start(f32[9,8,512]{2,1,0:T(8,128)} %get-tuple-element.81) | copy-start | bytes 442372
  159.8 5.0 %copy-start.34 = (f32[9,8,512]{2,1,0:T(8,128)S(1)}, f32[9,8,512]{2,1,0:T(8,128)}, u32[]{:S(2)}) copy-start(f32[9,8,512]{2,1,0:T(8,128)} %get-tuple-element.82) | copy-start | bytes 442372
  159.8 5.0 %copy-start.54 = (f32[8,512]{1,0:T(8,128)S(1)}, f32[8,512]{1,0:T(8,128)}, u32[]{:S(2)}) copy-start(f32[8,512]{1,0:T(8,128)} %convert_element_type.23) | copy-start | bytes 49156
  159.9 5.0 %copy-start.55 = (f32[1,8,512]{2,1,0:T(8,128)S(1)}, f32[1,8,512]{2,1,0:T(8,128)}, u32[]{:S(2)}) copy-start(f32[1,8,512]{2,1,0:T(8,128)} %get-tuple-element.75) | copy-start | bytes 49156
  159.9 5.0 %copy-start.56 = (f32[1,8,512]{2,1,0:T(8,128)S(1)}, f32[1,8,512]{2,1,0:T(8,128)}, u32[]{:S(2)}) copy-start(f32[1,8,512]{2,1,0:T(8,128)} %get-tuple-element.76) | copy-start | bytes 49156
  159.9 5.0 %copy-start.57 = (f32[1,8,512]{2,1,0:T(8,128)S(1)}, f32[1,8,512]{2,1,0:T(8,128)}, u32[]{:S(2)}) copy-start(f32[1,8,512]{2,1,0:T(8,128)} %get-tuple-element.77) | copy-start | bytes 49156
  159.9 5.0 %copy-start.58 = (f32[1,8,512]{2,1,0:T(8,128)S(1)}, f32[1,8,512]{2,1,0:T(8,128)}, u32[]{:S(2)}) copy-start(f32[1,8,512]{2,1,0:T(8,128)} %get-tuple-element.78) | copy-start | bytes 49156
  161.6 4.3 %copy-start.61 = (s32[8,512]{1,0:T(8,128)S(1)}, s32[8,512]{1,0:T(8,128)}, u32[]{:S(2)}) copy-start(s32[8,512]{1,0:T(8,128)} %param.14) | copy-start | bytes 49156
  (30 other events, 66.0 us)
where the time goes:
time: 169 us; the launch traced here: 167 us
  starting transfers between devices  56.5 us (33%)
  other arithmetic  49.5 us (29%)
  local copies, waits for them, and re-layouts  42.5 us (25%)
  waiting for transfers between devices  14.1 us (8%)
  matrix products  3.01 us (2%)
    ppermute x7, starting transfers between devices, extended_2(): lax.ppermute(lax.slice_in_dim(block, 0, width, axis=dim), axis, backward)  45 us
    mul x2, other arithmetic, stencil(): north_grad = 0.5 * (above_row - below_row)  15.1 us
    ppermute x7, waiting for transfers between devices, extended_2(): lax.ppermute(lax.slice_in_dim(block, block.shape[dim] - width, None, axis...  11.5 us
    ppermute x7, starting transfers between devices, extended_2(): lax.ppermute(lax.slice_in_dim(block, block.shape[dim] - width, None, axis...  11.5 us
    concatenate x2, local copies, waits for them, and re-layouts, extended_2(): block = jnp.concatenate([low, block, high], axis=dim)  9.26 us
    slice x3, local copies, waits for them, and re-layouts, extended_2(): lax.slice_in_dim(block, block.shape[dim] - width, None, axis=dim)  7.5 us
    slice x2, local copies, waits for them, and re-layouts, vertical(): joined_quantities[:-1]  6.57 us
    unnamed x128, local copies, waits for them, and re-layouts  6.43 us
  transfers between devices with their start and end apart: 14, of which 3 were waited for; matrix products, arithmetic and copies ran while one was open for 25% of the time, Pallas kernels for 0%

commit v1 on v0

v1 whole, which is shorter than its diff:
```python
import jax
import jax.numpy as jnp
from jax import lax
from jax.experimental import pallas as pl
from jax.experimental.pallas import tpu as pltpu
from jax.sharding import PartitionSpec as P

F32 = jnp.float32
LEV, ROWS, COLS = 16, 16, 1024
OLEV, OROWS, OCOLS = 10, 8, 512
WIDE = COLS + 128
OWIDE = OCOLS + 128
ANY = pl.BlockSpec(memory_space=pl.ANY)
SMEM = pl.BlockSpec(memory_space=pltpu.SMEM)


def lanes():
    return lax.broadcasted_iota(jnp.int32, (8, 128), 1)


def sublanes():
    return lax.broadcasted_iota(jnp.int32, (8, 128), 0)


def pack_kernel(x, ex, air, flow, warm, pay_a, pay_b, swp, dg_a, dg_b, xt, ft, wt, packed, sems):
    comp = lax.axis_index("comp")
    tile = lax.axis_index("tile")
    even = tile % 2 == 0

    cs = pl.multiple_of((1 - comp) * (COLS - 128), 128)
    os_ = pl.multiple_of((1 - comp) * (OCOLS - 128), 128)
    loads = [
        pltpu.make_async_copy(x.at[:, :, :, pl.ds(cs, 128)], xt, sems.at[1]),
        pltpu.make_async_copy(flow.at[:, :, :, pl.ds(os_, 128)], ft, sems.at[2]),
        pltpu.make_async_copy(warm.at[:, pl.ds(os_, 128)], wt, sems.at[3]),
    ]

    def rows_to(pay, rows, edge, oedge, sem):
        out = []
        for d in range(2):
            for f in range(3):
                out.append((x.at[f, :, rows[d], :], pay.at[pl.ds((d * 3 + f) * 16, 16), :]))
        for f in range(3):
            out.append((x.at[f, 0, rows[2], :], pay.at[104 + f, :]))
        out.append((ex.at[edge, :], pay.at[107, :]))
        out.append((air.at[edge, :], pay.at[108, :]))
        for k in range(2):
            cols = pl.ds(k * OCOLS, OCOLS)
            out.append((flow.at[k, pl.ds(0, 8), oedge, :], pay.at[pl.ds(96, 8), cols]))
            for lv in (8, 9):
                out.append((flow.at[k, lv, oedge, :], pay.at[101 + lv, cols]))
        out.append((warm.at[oedge, :], pay.at[111, pl.ds(0, OCOLS)]))
        return [pltpu.make_async_copy(a, b, sem) for a, b in out]

    top = ((0, 1, 2), 0, 0)
    bottom = ((15, 14, 13), 15, 7)

    @pl.when(even)
    def _():
        for c in rows_to(pay_b, *top, sems.at[0]) + rows_to(pay_a, *bottom, sems.at[0]):
            c.start()

    @pl.when(jnp.logical_not(even))
    def _():
        for c in rows_to(pay_b, *bottom, sems.at[0]) + rows_to(pay_a, *top, sems.at[0]):
            c.start()

    for c in loads:
        c.start()
    for c in loads:
        c.wait()
    lane = lanes()
    back = 1 - comp
    for rt in range(2):
        acc = jnp.zeros((8, 128), F32)
        for g in range(48):
            v = xt[g // 16, g % 16, rt * 8 : rt * 8 + 8, :]
            v = pltpu.roll(v, (2 * g + 2 * back) % 128, 1)
            acc = jnp.where(lane // 2 == g, v, acc)
        packed[rt * 8 : rt * 8 + 8, :] = acc
    acc = jnp.zeros((8, 128), F32)
    for g in range(21):
        v = ft[g // 10, g % 10] if g < 20 else wt[...]
        v = pltpu.roll(v, g + back, 1)
        acc = jnp.where(lane == g, v, acc)
    packed[16:24, :] = acc
    swp[...] = packed[...]
    first = jnp.where(even, 0, 8)
    dg_b[...] = packed[pl.ds(pl.multiple_of(first, 8), 8), :]
    dg_a[...] = packed[pl.ds(pl.multiple_of(8 - first, 8), 8), :]
    for c in rows_to(pay_b, *top, sems.at[0]) + rows_to(pay_a, *bottom, sems.at[0]):
        c.wait()


def pack(x, ex, air, flow, warm):
    vm = pl.BlockSpec(memory_space=pltpu.VMEM)
    sds = jax.ShapeDtypeStruct
    return pl.pallas_call(
        pack_kernel,
        out_shape=(
            sds((112, COLS), F32),
            sds((112, COLS), F32),
            sds((24, 128), F32),
            sds((8, 128), F32),
            sds((8, 128), F32),
        ),
        in_specs=[ANY] * 5,
        out_specs=(ANY, ANY, vm, vm, vm),
        scratch_shapes=[
            pltpu.VMEM((3, LEV, ROWS, 128), F32),
            pltpu.VMEM((2, OLEV, OROWS, 128), F32),
            pltpu.VMEM((OROWS, 128), F32),
            pltpu.VMEM((24, 128), F32),
            pltpu.SemaphoreType.DMA((4,)),
        ],
        compiler_params=pltpu.CompilerParams(vmem_limit_bytes=48 << 20),
        name="pack",
    )(x, ex, air, flow, warm)


def substep(src, level, tiles, lane, sub, store):
    up_l = jnp.maximum(level - 1, 0)
    dn_l = jnp.minimum(level + 1, LEV - 1)
    c, east, west, down, up = {}, {}, {}, {}, {}

    def need(lt):
        lt = lt % 9
        if (0, 0, lt) in c:
            return
        for f in range(3):
            for rt in range(3):
                v = src[f, level, rt * 8 : rt * 8 + 8, lt * 128 : lt * 128 + 128]
                c[f, rt, lt] = v
                if rt in tiles:
                    east[f, rt, lt] = pltpu.roll(v, 1, 1)
                    west[f, rt, lt] = pltpu.roll(v, 127, 1)
                up[f, rt, lt] = pltpu.roll(v, 1, 0)
                down[f, rt, lt] = pltpu.roll(v, 7, 0)

    need(8)
    need(0)
    for lt in range(9):
        need(lt + 1)
        for rt in tiles:
            left, right, prev, nxt, vert, four = {}, {}, {}, {}, {}, {}
            for f in range(3):
                left[f] = jnp.where(lane == 0, east[f, rt, (lt - 1) % 9], east[f, rt, lt])
                right[f] = jnp.where(lane == 127, west[f, rt, (lt + 1) % 9], west[f, rt, lt])
                prev[f] = jnp.where(sub == 0, up[f, (rt - 1) % 3, lt], up[f, rt, lt])
                nxt[f] = jnp.where(sub == 7, down[f, (rt + 1) % 3, lt], down[f, rt, lt])
                rows, cols = slice(rt * 8, rt * 8 + 8), slice(lt * 128, lt * 128 + 128)
                vert[f] = src[f, up_l, rows, cols] + src[f, dn_l, rows, cols]
                four[f] = 2.0 * ((left[f] + right[f]) + (prev[f] + nxt[f])) + vert[f]
            e = 0.06 * c[1, rt, lt] + 0.1 * (four[0] + (left[2] - right[2]))
            n = 0.1 * (four[1] + (prev[2] - nxt[2])) - 0.06 * c[0, rt, lt]
            h = 0.1 * (four[2] + (left[0] - right[0]) + (prev[1] - nxt[1]))
            store(rt, lt, (e, n, h))


def main_kernel(
    x, ex, air, flow, warm, water, part, tally, wgt, pay_a, pay_b, swp, dg_a, dg_b,
    out_x, out_flow, out_warm,
    s0, s1, s2, fl, coef, blocks, wv, res, oc, mask, of, ow, small, xsem, sems, wsem, osem,
):
    comp = lax.axis_index("comp")
    tile = lax.axis_index("tile")
    even = tile % 2 == 0
    lane, sub = lanes(), sublanes()

    wcopy = pltpu.make_async_copy(wgt, wv, wsem)
    xcopies = [
        pltpu.make_async_copy(x.at[f], s0.at[f, :, pl.ds(0, 16), pl.ds(0, COLS)], xsem.at[f])
        for f in range(3)
    ]
    for c in xcopies:
        c.start()

    def halo(pay, rows, third, sem):
        out = []
        for d in range(2):
            for f in range(3):
                out.append(
                    (pay.at[pl.ds((d * 3 + f) * 16, 16), :], s0.at[f, :, rows[d], pl.ds(0, COLS)])
                )
        for f in range(3):
            out.append((pay.at[104 + f, :], s0.at[f, 0, rows[2], pl.ds(0, COLS)]))
        to = pl.ds(0, OCOLS)
        for k in range(2):
            out.append((pay.at[107 + k, :], coef.at[k, rows[0], :]))
            cols = pl.ds(k * OCOLS, OCOLS)
            out.append((pay.at[pl.ds(96, 8), cols], oc.at[pl.ds(k * 10, 8), third, to]))
            for lv in (8, 9):
                out.append((pay.at[101 + lv, cols], oc.at[k * 10 + lv, third, to]))
        out.append((pay.at[111, to], oc.at[20, third, to]))
        return [pltpu.make_async_copy(a, b, sem) for a, b in out]

    above = ((23, 22, 21), 8)
    below = ((16, 17, 18), 15)
    smalls = [
        pltpu.make_async_copy(swp, small.at[pl.ds(0, 24), :], sems.at[1]),
        pltpu.make_async_copy(dg_a, small.at[pl.ds(24, 8), :], sems.at[1]),
        pltpu.make_async_copy(dg_b, small.at[pl.ds(32, 8), :], sems.at[1]),
    ]
    own = [
        pltpu.make_async_copy(ex, coef.at[0, pl.ds(0, 16), :], sems.at[2]),
        pltpu.make_async_copy(air, coef.at[1, pl.ds(0, 16), :], sems.at[2]),
        pltpu.make_async_copy(flow.at[0], oc.at[pl.ds(0, 10), pl.ds(0, 8), pl.ds(0, OCOLS)], sems.at[2]),
        pltpu.make_async_copy(flow.at[1], oc.at[pl.ds(10, 10), pl.ds(0, 8), pl.ds(0, OCOLS)], sems.at[2]),
        pltpu.make_async_copy(warm, oc.at[20, pl.ds(0, 8), pl.ds(0, OCOLS)], sems.at[2]),
        pltpu.make_async_copy(water, mask, sems.at[2]),
    ]

    @pl.when(even)
    def _():
        for c in halo(pay_b, *above, sems.at[0]) + halo(pay_a, *below, sems.at[0]):
            c.start()

    @pl.when(jnp.logical_not(even))
    def _():
        for c in halo(pay_a, *above, sems.at[0]) + halo(pay_b, *below, sems.at[0]):
            c.start()

    for c in smalls + own:
        c.start()
    wcopy.start()

    for c in smalls:
        c.wait()
    has_above = tile > 0
    has_below = tile < lax.axis_size("tile") - 1
    row_ok = jnp.where(sub >= 4, has_above.astype(jnp.int32), has_below.astype(jnp.int32)) > 0
    edge2 = jnp.where(comp == 0, lane, 127 - lane) < 2
    edge1 = jnp.where(comp == 0, lane, 127 - lane) < 1
    top_dg = jnp.where(even, 32, 24)
    corner = jnp.where(
        sub < 4,
        small[pl.ds(pl.multiple_of(56 - top_dg, 8), 8), :],
        small[pl.ds(pl.multiple_of(top_dg, 8), 8), :],
    )
    for g in range(48):
        shift = (128 - 2 * g + 126 * comp) % 128
        for rt in range(3):
            v = small[rt * 8 : rt * 8 + 8, :] if rt < 2 else corner
            ok = edge2 if rt < 2 else edge2 & row_ok
            s0[g // 16, g % 16, rt * 8 : rt * 8 + 8, COLS:WIDE] = jnp.where(
                ok, pltpu.roll(v, shift, 1), 0.0
            )

    for c in xcopies:
        c.wait()
    for c in halo(pay_b, *above, sems.at[0]) + halo(pay_a, *below, sems.at[0]):
        c.wait()
    for c in own:
        c.wait()

    @pl.when(jnp.logical_not(has_above & has_below))
    def _():
        def clear(g, _):
            for lt in range(8):
                cols = slice(lt * 128, lt * 128 + 128)
                for f in range(3):
                    s0[f, g, 16:24, cols] = jnp.where(row_ok, s0[f, g, 16:24, cols], 0.0)
            return 0

        lax.fori_loop(0, LEV, clear, 0)

        def oclear(g, _):
            for lt in range(4):
                cols = slice(lt * 128, lt * 128 + 128)
                keep = jnp.where(sub < 4, has_above.astype(jnp.int32), has_below.astype(jnp.int32)) > 0
                oc[g, 8:16, cols] = jnp.where(keep, oc[g, 8:16, cols], 0.0)
            return 0

        lax.fori_loop(0, 21, oclear, 0)

    def first(level, _):
        def store(rt, lt, new):
            rows, cols = slice(rt * 8, rt * 8 + 8), slice(lt * 128, lt * 128 + 128)
            for f in range(3):
                v = new[f]
                if lt == 8:
                    v = jnp.where(edge1 & row_ok if rt == 2 else edge1, v, 0.0)
                elif rt == 2:
                    v = jnp.where(row_ok, v, 0.0)
                s1[f, level, rows, cols] = v

        substep(s0, level, (0, 1, 2), lane, sub, store)
        return 0

    lax.fori_loop(0, LEV, first, 0)

    def out_copy(level):
        return pltpu.make_async_copy(s2.at[:, level], out_x.at[:, level], osem)

    def put_level0(rt, lt, new):
        rows, cols = slice(rt * 8, rt * 8 + 8), slice(lt * 128, lt * 128 + 128)
        if lt == 8:
            return
        for f in range(3):
            if rt < 2:
                s2[f, 0, rows, cols] = new[f]
        e, n, h = new
        mult = coef[0, rows, cols] * jnp.sqrt(e * e + n * n + 0.25)
        for f, v in enumerate((mult * e, mult * n, mult * (coef[1, rows, cols] - h))):
            hi = v.astype(jnp.bfloat16).astype(F32)
            blocks[pl.ds(rt * 512 + lt * 8 + f, 8, stride=64), :] = hi
            blocks[pl.ds(rt * 512 + lt * 8 + 3 + f, 8, stride=64), :] = v - hi
        blocks[pl.ds(rt * 512 + lt * 8 + 6, 8, stride=64), :] = jnp.ones((8, 128), F32)
        blocks[pl.ds(rt * 512 + lt * 8 + 7, 8, stride=64), :] = jnp.zeros((8, 128), F32)

    substep(s1, 0, (0, 1, 2), lane, sub, put_level0)
    out_copy(0).start()

    def second(level, _):
        def store(rt, lt, new):
            if lt == 8:
                return
            rows, cols = slice(rt * 8, rt * 8 + 8), slice(lt * 128, lt * 128 + 128)
            for f in range(3):
                s2[f, level, rows, cols] = new[f]

        substep(s1, level, (0, 1), lane, sub, store)
        out_copy(level).start()
        return 0

    lax.fori_loop(1, LEV, second, 0)

    wcopy.wait()
    base = tile * 128

    def remap(g, _):
        live = tally[g]
        parts = []
        for s in range(4):
            p = part[g, s] - base
            p = jnp.where(p < 0, p + 192, p)
            row = pl.multiple_of(p * 8, 8)
            v = blocks[pl.ds(row, 8), :]
            parts.append(v * jnp.where(s < live, 1.0, 0.0))
        lhs = jnp.concatenate(parts, axis=1).astype(jnp.bfloat16)
        rhs = wv[g].reshape(512, 128)
        res[pl.ds(pl.multiple_of(g * 8, 8), 8), :] = jnp.dot(lhs, rhs, preferred_element_type=F32)
        return 0

    lax.fori_loop(0, 32, remap, 0, unroll=4)

    def unpack_ocean():
        for g in range(21):
            shift = (128 - g + 127 * comp) % 128
            v = pltpu.roll(small[16:24, :], shift, 1)
            oc[g, 0:8, OCOLS:OWIDE] = jnp.where(edge1, v, 0.0)

    unpack_ocean()

    def around(g, lt):
        cols = slice(lt * 128, lt * 128 + 128)
        c = oc[g, 0:8, cols]
        hv = oc[g, 8:16, cols]
        lo, hi = (lt - 1) % 5, lt + 1
        left = jnp.where(lane == 0, pltpu.roll(oc[g, 0:8, lo * 128 : lo * 128 + 128], 1, 1), pltpu.roll(c, 1, 1))
        right = jnp.where(lane == 127, pltpu.roll(oc[g, 0:8, hi * 128 : hi * 128 + 128], 127, 1), pltpu.roll(c, 127, 1))
        prev = jnp.where(sub == 0, hv, pltpu.roll(c, 1, 0))
        nxt = jnp.where(sub == 7, hv, pltpu.roll(c, 7, 0))
        return c, left, right, prev, nxt

    for lt in range(4):
        cols = slice(lt * 128, lt * 128 + 128)
        m = mask[:, cols].astype(F32)
        den = res[pl.ds(lt * 8 + 6, 8, stride=32), :]
        rem = [
            (res[pl.ds(lt * 8 + f, 8, stride=32), :] + res[pl.ds(lt * 8 + f + 3, 8, stride=32), :]) / den
            for f in range(3)
        ]
        for k in range(2):
            for lv in range(10):
                g = k * 10 + lv
                c, left, right, prev, nxt = around(g, lt)
                other = oc[(1 - k) * 10 + lv, 0:8, cols]
                vert = oc[k * 10 + max(lv - 1, 0), 0:8, cols] + oc[k * 10 + min(lv + 1, 9), 0:8, cols]
                v = 0.2 * ((left + right) + (prev + nxt)) + 0.1 * vert
                v = v + (0.06 if k == 0 else -0.06) * other
                if lv == 0:
                    v = v + 0.2 * rem[k]
                of[k, lv, :, cols] = m * v
        c, left, right, prev, nxt = around(20, lt)
        lap = (left + right) + (prev + nxt) - 4.0 * c
        carried = oc[0, 0:8, cols] * (0.5 * (right - left)) + oc[10, 0:8, cols] * (0.5 * (nxt - prev))
        ow[:, cols] = c + (m * 0.2) * (rem[2] - carried + 0.5 * lap)
    tail = [
        pltpu.make_async_copy(of, out_flow, sems.at[3]),
        pltpu.make_async_copy(ow, out_warm, sems.at[3]),
    ]
    for c in tail:
        c.start()
    for c in tail:
        c.wait()
    lax.fori_loop(0, LEV, lambda l, _: (out_copy(l).wait(), 0)[1], 0)


def advance_all(x, ex, air, flow, warm, water, part, tally, wgt, halos):
    sds = jax.ShapeDtypeStruct
    return pl.pallas_call(
        main_kernel,
        out_shape=(sds(x.shape, F32), sds(flow.shape, F32), sds(warm.shape, F32)),
        in_specs=[ANY] * 6 + [SMEM] * 2 + [ANY] * 6,
        out_specs=(ANY, ANY, ANY),
        scratch_shapes=[
            pltpu.VMEM((3, LEV, 24, WIDE), F32),
            pltpu.VMEM((3, LEV, 24, WIDE), F32),
            pltpu.VMEM((3, LEV, ROWS, COLS), F32),
            pltpu.VMEM((8, 128), F32),
            pltpu.VMEM((2, 24, COLS), F32),
            pltpu.VMEM((24 * 64, 128), F32),
            pltpu.VMEM((32, 4, 128, 128), jnp.bfloat16),
            pltpu.VMEM((256, 128), F32),
            pltpu.VMEM((21, 16, OWIDE), F32),
            pltpu.VMEM((OROWS, OCOLS), jnp.int32),
            pltpu.VMEM((2, OLEV, OROWS, OCOLS), F32),
            pltpu.VMEM((OROWS, OCOLS), F32),
            pltpu.VMEM((40, 128), F32),
            pltpu.SemaphoreType.DMA((3,)),
            pltpu.SemaphoreType.DMA((4,)),
            pltpu.SemaphoreType.DMA,
            pltpu.SemaphoreType.DMA,
        ],
        compiler_params=pltpu.CompilerParams(vmem_limit_bytes=48 << 20),
        name="advance_all",
    )(x, ex, air, flow, warm, water, part, tally, wgt, *halos)


def exchange(pay_a, pay_b, swp, dg_a, dg_b):
    tiles = lax.axis_size("tile")
    pair_a = [t ^ 1 for t in range(tiles)]
    pair_b = [t if t in (0, tiles - 1) else (t - 1 if t % 2 == 0 else t + 1) for t in range(tiles)]

    def straight(v, pair):
        return lax.ppermute(v, "tile", list(enumerate(pair)))

    def diagonal(v, pair):
        perm = [(c * tiles + t, (1 - c) * tiles + p) for c in range(2) for t, p in enumerate(pair)]
        return lax.ppermute(v, ("comp", "tile"), perm)

    got_b = straight(pay_b, pair_b)
    got_a = straight(pay_a, pair_a)
    return (
        got_a,
        got_b,
        lax.ppermute(swp, "comp", [(0, 1), (1, 0)]),
        diagonal(dg_a, pair_a),
        diagonal(dg_b, pair_b),
    )


def shards(x, ex, air, flow, warm, water, part, tally, wgt):
    halos = exchange(*pack(x, ex, air, flow, warm))
    return advance_all(x, ex, air, flow, warm, water, part, tally, wgt, halos)


def solution(mesh):
    placed = (
        P(None, None, "tile", "comp"),
        P("tile", "comp"),
        P("tile", "comp"),
        P(None, None, "tile", "comp"),
        P("tile", "comp"),
        P("tile", "comp"),
        P(("comp", "tile"), None),
        P(("comp", "tile")),
        P(("comp", "tile"), None, None, None),
    )
    return jax.shard_map(
        shards,
        mesh=mesh,
        in_specs=placed,
        out_specs=(P(None, None, "tile", "comp"), P(None, None, "tile", "comp"), P("tile", "comp")),
        check_vma=False,
    )
```

time: 169 us -> 46 us (0.27)
  the two profiles are of different devices: /device:TPU:24 before, /device:TPU:8 now
where the time goes in v1:
time: 46 us; the launch traced here: 45.3 us
  Pallas kernels  16.1 us (35%)
  starting transfers between devices  15.5 us (34%)
  local copies, waits for them, and re-layouts  9.55 us (21%)
  waiting for transfers between devices  3.42 us (7%)
  between operations  0.72 us (2%)
    pallas_call x1, Pallas kernels, advance_all(): pl.pallas_call(main_kernel, out_shape=(sds(x.shape, F32), sds(flow.shape,...  14.5 us
    ppermute x2, starting transfers between devices, straight(): return lax.ppermute(v, 'tile', list(enumerate(pair)))  10 us
    unnamed x27, local copies, waits for them, and re-layouts  9.55 us
    ppermute x2, waiting for transfers between devices, diagonal(): return lax.ppermute(v, ('comp', 'tile'), perm)  3.41 us
    ppermute x2, starting transfers between devices, diagonal(): return lax.ppermute(v, ('comp', 'tile'), perm)  2.79 us
    ppermute x1, starting transfers between devices, exchange(): lax.ppermute(swp, 'comp', [(0, 1), (1, 0)])  2.68 us
    pallas_call x1, Pallas kernels, pack(): pl.pallas_call(pack_kernel, out_shape=(sds((112, COLS), F32), sds((112, C...  1.6 us
  transfers between devices with their start and end apart: 5, of which 2 were waited for; matrix products, arithmetic and copies ran while one was open for 3% of the time, Pallas kernels for 0%

profile of v1, /device:TPU:8, one launch (start us, length us, event | category | flops | bytes accessed | tf_op | source)
XLA Modules:
  0.0 45.3 jit_solution(9314124027143661859)
XLA Ops:
  0.6 0.0 copy-start
  0.6 1.9 %copy-done = f32[3,16,16,1024]{3,2,1,0:T(8,128)S(1)} copy-done((f32[3,16,16,1024]{3,2,1,0:T(8,128)S(1)}, f32[3,16,16,1024]{3,2,1,0:T(8,128)}, u32[]{:S(2)}) %copy-start) | copy-done | bytes 3145752
  2.5 0.0 copy-start.2
  2.5 1.0 %copy-done.2 = f32[2,10,8,512]{3,2,1,0:T(8,128)S(1)} copy-done((f32[2,10,8,512]{3,2,1,0:T(8,128)S(1)}, f32[2,10,8,512]{3,2,1,0:T(8,128)}, u32[]{:S(2)}) %copy-start.2) | copy-done | bytes 327704
  3.5 0.0 copy-start.4
  3.5 0.8 %copy-done.4 = f32[16,1024]{1,0:T(8,128)S(1)} copy-done((f32[16,1024]{1,0:T(8,128)S(1)}, f32[16,1024]{1,0:T(8,128)}, u32[]{:S(2)}) %copy-start.4) | copy-done | bytes 65560
  4.3 0.0 copy-start.6
  4.3 0.8 %copy-done.6 = f32[16,1024]{1,0:T(8,128)S(1)} copy-done((f32[16,1024]{1,0:T(8,128)S(1)}, f32[16,1024]{1,0:T(8,128)}, u32[]{:S(2)}) %copy-start.6) | copy-done | bytes 65560
  5.2 0.0 copy-start.8
  5.2 0.7 %copy-done.8 = f32[8,512]{1,0:T(8,128)S(1)} copy-done((f32[8,512]{1,0:T(8,128)S(1)}, f32[8,512]{1,0:T(8,128)}, u32[]{:S(2)}) %copy-start.8) | copy-done | bytes 16408
  5.9 0.0 copy-start.1
  5.9 0.0 copy-start.3
  5.9 0.0 copy-start.5
  5.9 0.0 copy-start.9
  5.9 1.6 %pack.1 = (f32[112,1024]{1,0:T(8,128)}, f32[112,1024]{1,0:T(8,128)}, f32[24,128]{1,0:T(8,128)}, f32[8,128]{1,0:T(8,128)}, f32[8,128]{1,0:T(8,128)}) custom-call(f32[3,16,16,1024]{3,2,1,0:T(8,128)S(1)} %copy-done, f32[16,1024]{1,0:T(8,128)S(1)} %copy-done.4, f32[16,1024]{1,0:T(8,128)S(1)} %copy-done.6, f32[2,10,8,512]{3,2,1,0:T(8,128)S(1)} %copy-done.2, ...), custom_call_target="tpu_custom_call" | custom-call | tf_op jit(solution)/shard_map/pack/pallas_call | solution.py:98
  7.5 0.1 collective-permute-start
  7.6 9.9 %collective-permute-start.1 = (f32[112,1024]{1,0:T(8,128)}, f32[112,1024]{1,0:T(8,128)}, u32[]{:S(2)}, u32[]{:S(2)}) collective-permute-start(f32[112,1024]{1,0:T(8,128)} %get-tuple-element.9), channel_id=1, source_target_pairs={{0,0},{1,2},{2,1},{3,4},{4,3},{5,6},{6,5},{7,8},{8,7},{9,10},{10,9... | collective-permute-start | bytes 1376264 | tf_op jit(solution)/shard_map/ppermute | solution.py:437
  17.6 2.7 %collective-permute-start.2 = (f32[24,128]{1,0:T(8,128)}, f32[24,128]{1,0:T(8,128)}, u32[]{:S(2)}, u32[]{:S(2)}) collective-permute-start(f32[24,128]{1,0:T(8,128)} %get-tuple-element.10), channel_id=1, source_target_pairs={{0,128},{128,0},{1,129},{129,1},{2,130},{130,2},{3,131},{131,3},{4... | collective-permute-start | bytes 36872 | tf_op jit(solution)/shard_map/ppermute | solution.py:448
  20.2 0.0 collective-permute-start.3
  20.2 2.8 %collective-permute-start.4 = (f32[8,128]{1,0:T(8,128)}, f32[8,128]{1,0:T(8,128)}, u32[]{:S(2)}, u32[]{:S(2)}) collective-permute-start(f32[8,128]{1,0:T(8,128)} %get-tuple-element.12), channel_id=1, source_target_pairs={{0,128},{1,130},{2,129},{3,132},{4,131},{5,134},{6,133},{7,136},{8... | collective-permute-start | bytes 12296 | tf_op jit(solution)/shard_map/ppermute | solution.py:441
  23.0 1.4 %copy.12.part = s32[32,4]{1,0:T(8,128)} copy(s32[32,4]{0,1:T(4,128)} %param.15) | data formatting | bytes 1024 | tf_op args[6]
  24.4 0.7 %collective-permute-done.3.dg_a = f32[8,128]{1,0:T(8,128)} collective-permute-done((f32[8,128]{1,0:T(8,128)}, f32[8,128]{1,0:T(8,128)}, u32[]{:S(2)}, u32[]{:S(2)}) %collective-permute-start.3) | collective-permute-done | bytes 4128 | tf_op jit(solution)/shard_map/ppermute | solution.py:441
  25.1 2.7 %collective-permute-done.4.dg_b = f32[8,128]{1,0:T(8,128)} collective-permute-done((f32[8,128]{1,0:T(8,128)}, f32[8,128]{1,0:T(8,128)}, u32[]{:S(2)}, u32[]{:S(2)}) %collective-permute-start.4) | collective-permute-done | bytes 4128 | tf_op jit(solution)/shard_map/ppermute | solution.py:441
  27.8 0.0 collective-permute-done.2.swp
  27.8 0.0 collective-permute-done.pay_a
  27.8 0.0 collective-permute-done.1.pay_b
  27.8 0.0 copy-done.1
  27.8 0.0 copy-done.3
  27.8 0.0 copy-done.5
  27.8 0.0 copy-done.9
  27.9 0.0 copy-start.7
  27.9 0.8 %copy-done.7 = f32[16,1024]{1,0:T(8,128)S(1)} copy-done((f32[16,1024]{1,0:T(8,128)S(1)}, f32[16,1024]{1,0:T(8,128)}, u32[]{:S(2)}) %copy-start.7) | copy-done | bytes 65560
  28.7 0.0 copy-start.10
  28.7 0.7 %copy-done.10 = s32[32,4]{1,0:T(8,128)S(1)} copy-done((s32[32,4]{1,0:T(8,128)S(1)}, s32[32,4]{1,0:T(8,128)}, u32[]{:S(2)}) %copy-start.10) | copy-done | bytes 536
  29.4 0.0 copy-start.11
  29.4 0.7 %copy-done.11 = s32[8,512]{1,0:T(8,128)S(1)} copy-done((s32[8,512]{1,0:T(8,128)S(1)}, s32[8,512]{1,0:T(8,128)}, u32[]{:S(2)}) %copy-start.11) | copy-done | bytes 16408
  30.1 0.0 copy-start.12
  30.1 0.7 %copy-done.12 = s32[32]{0:T(128)S(1)} copy-done((s32[32]{0:T(128)S(1)}, s32[32]{0:T(128)}, u32[]{:S(2)}) %copy-start.12) | copy-done | bytes 152
  30.8 14.5 %advance_all.1 = (f32[3,16,16,1024]{3,2,1,0:T(8,128)}, f32[2,10,8,512]{3,2,1,0:T(8,128)}, f32[8,512]{1,0:T(8,128)}) custom-call(f32[3,16,16,1024]{3,2,1,0:T(8,128)S(1)} %copy-done.1, f32[16,1024]{1,0:T(8,128)S(1)} %copy-done.5, f32[16,1024]{1,0:T(8,128)S(1)} %copy-done.7, f32[2,10,8,512]{3,2,1,0:T(8,128)S(1)} %copy-done.3, f32[8,512]{1,0:T(8,128)S(1)} %copy-done.9, ...), custom_call_target="tpu_custom_call" | custom-call | tf_op jit(solution)/shard_map/advance_all/pallas_call | solution.py:402
Async XLA Ops:
  0.6 1.9 %copy-start = (f32[3,16,16,1024]{3,2,1,0:T(8,128)S(1)}, f32[3,16,16,1024]{3,2,1,0:T(8,128)}, u32[]{:S(2)}) copy-start(f32[3,16,16,1024]{3,2,1,0:T(8,128)} %x.3) | copy-start | bytes 9437188
  2.5 1.0 %copy-start.2 = (f32[2,10,8,512]{3,2,1,0:T(8,128)S(1)}, f32[2,10,8,512]{3,2,1,0:T(8,128)}, u32[]{:S(2)}) copy-start(f32[2,10,8,512]{3,2,1,0:T(8,128)} %flow.3) | copy-start | bytes 983044
  3.5 0.8 %copy-start.4 = (f32[16,1024]{1,0:T(8,128)S(1)}, f32[16,1024]{1,0:T(8,128)}, u32[]{:S(2)}) copy-start(f32[16,1024]{1,0:T(8,128)} %ex.3) | copy-start | bytes 196612
  4.3 0.8 %copy-start.6 = (f32[16,1024]{1,0:T(8,128)S(1)}, f32[16,1024]{1,0:T(8,128)}, u32[]{:S(2)}) copy-start(f32[16,1024]{1,0:T(8,128)} %air.3) | copy-start | bytes 196612
  5.2 0.7 %copy-start.8 = (f32[8,512]{1,0:T(8,128)S(1)}, f32[8,512]{1,0:T(8,128)}, u32[]{:S(2)}) copy-start(f32[8,512]{1,0:T(8,128)} %warm.3) | copy-start | bytes 49156
  5.9 21.9 %copy-start.1 = (f32[3,16,16,1024]{3,2,1,0:T(8,128)S(1)}, f32[3,16,16,1024]{3,2,1,0:T(8,128)}, u32[]{:S(2)}) copy-start(f32[3,16,16,1024]{3,2,1,0:T(8,128)} %x.3) | copy-start | bytes 9437188
  5.9 21.9 %copy-start.3 = (f32[2,10,8,512]{3,2,1,0:T(8,128)S(1)}, f32[2,10,8,512]{3,2,1,0:T(8,128)}, u32[]{:S(2)}) copy-start(f32[2,10,8,512]{3,2,1,0:T(8,128)} %flow.3) | copy-start | bytes 983044
  5.9 21.9 %copy-start.5 = (f32[16,1024]{1,0:T(8,128)S(1)}, f32[16,1024]{1,0:T(8,128)}, u32[]{:S(2)}) copy-start(f32[16,1024]{1,0:T(8,128)} %ex.3) | copy-start | bytes 196612
  5.9 22.0 %copy-start.9 = (f32[8,512]{1,0:T(8,128)S(1)}, f32[8,512]{1,0:T(8,128)}, u32[]{:S(2)}) copy-start(f32[8,512]{1,0:T(8,128)} %warm.3) | copy-start | bytes 49156
  7.5 20.3 %collective-permute-start = (f32[112,1024]{1,0:T(8,128)}, f32[112,1024]{1,0:T(8,128)}, u32[]{:S(2)}, u32[]{:S(2)}) collective-permute-start(f32[112,1024]{1,0:T(8,128)} %get-tuple-element.8), channel_id=1, source_target_pairs={{0,1},{1,0},{2,3},{3,2},{4,5},{5,4},{6,7},{7,6},{8,9},{9,8},{10,11... | collective-permute-start | bytes 1376264 | tf_op jit(solution)/shard_map/ppermute | solution.py:437
  7.6 20.2 %collective-permute-start.1 = (f32[112,1024]{1,0:T(8,128)}, f32[112,1024]{1,0:T(8,128)}, u32[]{:S(2)}, u32[]{:S(2)}) collective-permute-start(f32[112,1024]{1,0:T(8,128)} %get-tuple-element.9), channel_id=1, source_target_pairs={{0,0},{1,2},{2,1},{3,4},{4,3},{5,6},{6,5},{7,8},{8,7},{9,10},{10,9... | collective-permute-start | bytes 1376264 | tf_op jit(solution)/shard_map/ppermute | solution.py:437
  17.6 10.2 %collective-permute-start.2 = (f32[24,128]{1,0:T(8,128)}, f32[24,128]{1,0:T(8,128)}, u32[]{:S(2)}, u32[]{:S(2)}) collective-permute-start(f32[24,128]{1,0:T(8,128)} %get-tuple-element.10), channel_id=1, source_target_pairs={{0,128},{128,0},{1,129},{129,1},{2,130},{130,2},{3,131},{131,3},{4... | collective-permute-start | bytes 36872 | tf_op jit(solution)/shard_map/ppermute | solution.py:448
  20.2 4.9 %collective-permute-start.3 = (f32[8,128]{1,0:T(8,128)}, f32[8,128]{1,0:T(8,128)}, u32[]{:S(2)}, u32[]{:S(2)}) collective-permute-start(f32[8,128]{1,0:T(8,128)} %get-tuple-element.11), channel_id=1, source_target_pairs={{0,129},{1,128},{2,131},{3,130},{4,133},{5,132},{6,135},{7,134},{8... | collective-permute-start | bytes 12296 | tf_op jit(solution)/shard_map/ppermute | solution.py:441
  20.2 7.6 %collective-permute-start.4 = (f32[8,128]{1,0:T(8,128)}, f32[8,128]{1,0:T(8,128)}, u32[]{:S(2)}, u32[]{:S(2)}) collective-permute-start(f32[8,128]{1,0:T(8,128)} %get-tuple-element.12), channel_id=1, source_target_pairs={{0,128},{1,130},{2,129},{3,132},{4,131},{5,134},{6,133},{7,136},{8... | collective-permute-start | bytes 12296 | tf_op jit(solution)/shard_map/ppermute | solution.py:441
  27.9 0.8 %copy-start.7 = (f32[16,1024]{1,0:T(8,128)S(1)}, f32[16,1024]{1,0:T(8,128)}, u32[]{:S(2)}) copy-start(f32[16,1024]{1,0:T(8,128)} %air.3) | copy-start | bytes 196612
  28.7 0.7 %copy-start.10 = (s32[32,4]{1,0:T(8,128)S(1)}, s32[32,4]{1,0:T(8,128)}, u32[]{:S(2)}) copy-start(s32[32,4]{1,0:T(8,128)} %copy.12.part) | copy-start | bytes 1540
  29.4 0.7 %copy-start.11 = (s32[8,512]{1,0:T(8,128)S(1)}, s32[8,512]{1,0:T(8,128)}, u32[]{:S(2)}) copy-start(s32[8,512]{1,0:T(8,128)} %water.1) | copy-start | bytes 49156
  30.1 0.7 %copy-start.12 = (s32[32]{0:T(128)S(1)}, s32[32]{0:T(128)}, u32[]{:S(2)}) copy-start(s32[32]{0:T(128)} %tally.1) | copy-start | bytes 388

commit v2 on v1

v2 whole, which is shorter than its diff:
```python
import functools

import jax
import jax.numpy as jnp
from jax import lax
from jax.experimental import pallas as pl
from jax.experimental.pallas import tpu as pltpu
from jax.sharding import PartitionSpec as P

F32 = jnp.float32
VMEM_ALL = 63 << 20
LEV, ROWS, COLS = 16, 16, 1024
OLEV, OROWS, OCOLS = 10, 8, 512
WIDE = COLS + 128
OWIDE = OCOLS + 128
ANY = pl.BlockSpec(memory_space=pl.ANY)
SMEM = pl.BlockSpec(memory_space=pltpu.SMEM)


def lanes():
    return lax.broadcasted_iota(jnp.int32, (8, 128), 1)


def sublanes():
    return lax.broadcasted_iota(jnp.int32, (8, 128), 0)


def sweep(src, level, up_l, dn_l, rts, lts, wrap, edge, store):
    lane, sub = lanes(), sublanes()
    c, east, west, down, up = {}, {}, {}, {}, {}
    every = range(3) if wrap else rts
    nl = 9 if wrap else 8
    nr = len(every)

    def need(lt):
        if (0, every[0], lt) in c:
            return
        for f in range(3):
            for rt in every:
                v = src[f, level, rt * 8 : rt * 8 + 8, lt * 128 : lt * 128 + 128]
                c[f, rt, lt] = v
                if rt in rts:
                    east[f, rt, lt] = pltpu.roll(v, 1, 1)
                    west[f, rt, lt] = pltpu.roll(v, 127, 1)
                up[f, rt, lt] = pltpu.roll(v, 1, 0)
                down[f, rt, lt] = pltpu.roll(v, 7, 0)

    if wrap:
        need(8)
    need(0)
    for lt in lts:
        if wrap or lt < nl - 1:
            need((lt + 1) % nl)
        for rt in rts:
            inner = {
                "left": wrap or lt > 0,
                "right": wrap or lt < nl - 1,
                "prev": wrap or rt > 0,
                "next": wrap or rt < nr - 1,
            }
            out = {k: None if v else edge(k, rt, lt) for k, v in inner.items()}
            left, right, prev, nxt, four = {}, {}, {}, {}, {}
            for f in range(3):
                o = {k: out[k][f] if out[k] is not None else None for k in out}
                if inner["left"]:
                    o["left"] = east[f, rt, (lt - 1) % nl]
                if inner["right"]:
                    o["right"] = west[f, rt, (lt + 1) % nl]
                if inner["prev"]:
                    o["prev"] = up[f, (rt - 1) % nr, lt]
                if inner["next"]:
                    o["next"] = down[f, (rt + 1) % nr, lt]
                left[f] = jnp.where(lane == 0, o["left"], east[f, rt, lt])
                right[f] = jnp.where(lane == 127, o["right"], west[f, rt, lt])
                prev[f] = jnp.where(sub == 0, o["prev"], up[f, rt, lt])
                nxt[f] = jnp.where(sub == 7, o["next"], down[f, rt, lt])
                rows, cols = slice(rt * 8, rt * 8 + 8), slice(lt * 128, lt * 128 + 128)
                vert = src[f, up_l, rows, cols] + src[f, dn_l, rows, cols]
                four[f] = 2.0 * ((left[f] + right[f]) + (prev[f] + nxt[f])) + vert
            e = 0.06 * c[1, rt, lt] + 0.1 * (four[0] + (left[2] - right[2]))
            n = 0.1 * (four[1] + (prev[2] - nxt[2])) - 0.06 * c[0, rt, lt]
            h = 0.1 * (four[2] + (left[0] - right[0]) + (prev[1] - nxt[1]))
            store(rt, lt, (e, n, h))


def sideways(v, sign):
    e, n, h = v
    return (0.1 * (2.0 * e + sign * h), 0.2 * n, 0.1 * (2.0 * h + sign * e))


def upright(v, sign):
    e, n, h = v
    return (0.2 * e, 0.1 * (2.0 * n + sign * h), 0.1 * (2.0 * h + sign * n))


def neighbours():
    tile = lax.axis_index("tile")
    return tile > 0, tile < lax.axis_size("tile") - 1


def share(early):
    place = lax.axis_index("tile") % 16
    cut = jnp.where(place == 0, LEV, jnp.where(place == 1, LEV // 2, 0))
    return (0, cut) if early else (cut, LEV)


def own_work(x, s1, s2, out_x, rb, cb, sem, ready, lo, hi):
    comp = lax.axis_index("comp")
    has_above, has_below = neighbours()
    zero = jnp.zeros((8, 128), F32)

    def first(level, _):
        ready(level)

        def store(rt, lt, new):
            for f in range(3):
                s1[f, level, rt * 8 : rt * 8 + 8, lt * 128 : lt * 128 + 128] = new[f]

        dn = jnp.minimum(level + 1, LEV - 1)
        sweep(x, level, jnp.maximum(level - 1, 0), dn, (0, 1), range(8), False, lambda *a: (zero,) * 3, store)
        return 0

    lax.fori_loop(jnp.maximum(lo - 1, 0), jnp.minimum(hi + 1, LEV), first, 0)
    gain = {
        "left": comp.astype(F32),
        "right": (1 - comp).astype(F32),
        "prev": has_above.astype(F32),
        "next": has_below.astype(F32),
    }

    def out_copy(level):
        return pltpu.make_async_copy(s2.at[:, level], out_x.at[:, level], sem)

    def second(level, _):
        def edge(kind, rt, lt):
            v = [x[f, level, rt * 8 : rt * 8 + 8, lt * 128 : lt * 128 + 128] for f in range(3)]
            put = sideways if kind in ("left", "right") else upright
            return [gain[kind] * w for w in put(v, -1.0 if kind in ("left", "prev") else 1.0)]

        def store(rt, lt, new):
            for f in range(3):
                s2[f, level, rt * 8 : rt * 8 + 8, lt * 128 : lt * 128 + 128] = new[f]

        dn = jnp.minimum(level + 1, LEV - 1)
        sweep(s1, level, jnp.maximum(level - 1, 0), dn, (0, 1), range(8), False, edge, store)
        out_copy(level).start()
        return 0

    lax.fori_loop(lo, hi, second, 0)
    es = pl.multiple_of((1 - comp) * (COLS - 128), 128)

    def kept(half):
        some = pl.ds(half * 8, 8)
        out = [pltpu.make_async_copy(s2.at[:, some, :, pl.ds(es, 128)], cb.at[:, some], sem)]
        for k, r in enumerate((0, 1, 15, 14)):
            for f in range(3):
                to = rb.at[pl.ds((k * 3 + f) * 16 + half * 8, 8), :]
                out.append(pltpu.make_async_copy(s2.at[f, some, r, :], to, sem))
        return out

    for half in range(2):

        @pl.when((lo <= half * 8) & (half * 8 < hi))
        def _():
            for c in kept(half):
                c.start()

    for half in range(2):

        @pl.when((lo <= half * 8) & (half * 8 < hi))
        def _():
            for c in kept(half):
                c.wait()

    lax.fori_loop(lo, hi, lambda l, _: (out_copy(l).wait(), 0)[1], 0)


def pack_kernel(
    x_in, ex_in, air_in, flow_in, warm_in,
    pay_up, pay_dn, swp,
    x, ex, air, flow, warm, packed, sems,
):
    comp = lax.axis_index("comp")
    cs = pl.multiple_of((1 - comp) * (COLS - 128), 128)
    os_ = pl.multiple_of((1 - comp) * (OCOLS - 128), 128)
    loads = [
        pltpu.make_async_copy(a, b, sems.at[1])
        for a, b in ((x_in, x), (ex_in, ex), (air_in, air), (flow_in, flow), (warm_in, warm))
    ]
    for c in loads:
        c.start()

    def rows_to(pay, rows, edge, oedge, sem):
        out = []
        for d in range(2):
            for f in range(3):
                out.append((x.at[f, :, rows[d], :], pay.at[pl.ds((d * 3 + f) * 16, 16), :]))
        for f in range(3):
            out.append((x.at[f, 0, rows[2], :], pay.at[104 + f, :]))
        out.append((ex.at[edge, :], pay.at[107, :]))
        out.append((air.at[edge, :], pay.at[108, :]))
        for k in range(2):
            cols = pl.ds(k * OCOLS, OCOLS)
            out.append((flow.at[k, pl.ds(0, 8), oedge, :], pay.at[pl.ds(96, 8), cols]))
            for lv in (8, 9):
                out.append((flow.at[k, lv, oedge, :], pay.at[101 + lv, cols]))
        out.append((warm.at[oedge, :], pay.at[111, pl.ds(0, OCOLS)]))
        return [pltpu.make_async_copy(a, b, sem) for a, b in out]

    top = ((0, 1, 2), 0, 0)
    bottom = ((15, 14, 13), 15, 7)

    for c in loads:
        c.wait()

    sends = rows_to(pay_up, *bottom, sems.at[0]) + rows_to(pay_dn, *top, sems.at[0])
    for c in sends:
        c.start()

    lane = lanes()
    back = 1 - comp
    for rt in range(2):
        acc = jnp.zeros((8, 128), F32)
        for g in range(48):
            v = x[g // 16, g % 16, rt * 8 : rt * 8 + 8, pl.ds(cs, 128)]
            v = pltpu.roll(v, (2 * g + 2 * back) % 128, 1)
            acc = jnp.where(lane // 2 == g, v, acc)
        packed[rt * 8 : rt * 8 + 8, :] = acc
    acc = jnp.zeros((8, 128), F32)
    for g in range(21):
        v = flow[g // 10, g % 10, :, pl.ds(os_, 128)] if g < 20 else warm[:, pl.ds(os_, 128)]
        v = pltpu.roll(v, g + back, 1)
        acc = jnp.where(lane == g, v, acc)
    packed[16:24, :] = acc
    swp[...] = packed[...]
    corners = [
        pltpu.make_async_copy(packed.at[pl.ds(8, 8), :], pay_up.at[pl.ds(112, 8), pl.ds(0, 128)], sems.at[0]),
        pltpu.make_async_copy(packed.at[pl.ds(0, 8), :], pay_dn.at[pl.ds(112, 8), pl.ds(0, 128)], sems.at[0]),
    ]
    for c in corners:
        c.start()
    for c in sends + corners:
        c.wait()


KEPT = ((3, LEV, ROWS, COLS), (192, COLS), (3, LEV, ROWS, 128))
STATE = pltpu.VMEM((3, LEV, ROWS, COLS), F32)


def pack(x, ex, air, flow, warm):
    vm = pl.BlockSpec(memory_space=pltpu.VMEM)
    sds = jax.ShapeDtypeStruct
    return pl.pallas_call(
        pack_kernel,
        out_shape=(
            sds((128, COLS), F32),
            sds((120, COLS), F32),
            sds((24, 128), F32),
        ),
        in_specs=[ANY] * 5,
        out_specs=(ANY, ANY, vm),
        scratch_shapes=[
            STATE,
            pltpu.VMEM((ROWS, COLS), F32),
            pltpu.VMEM((ROWS, COLS), F32),
            pltpu.VMEM((2, OLEV, OROWS, OCOLS), F32),
            pltpu.VMEM((OROWS, OCOLS), F32),
            pltpu.VMEM((24, 128), F32),
            pltpu.SemaphoreType.DMA((2,)),
        ],
        compiler_params=pltpu.CompilerParams(vmem_limit_bytes=VMEM_ALL),
        name="pack",
    )(x, ex, air, flow, warm)


def own_kernel(early, passed, x_in, *refs):
    out_x, rb, cb = refs[passed : passed + 3]
    x, s1, s2, sem, xsem = refs[-5:]
    lo, hi = share(early)

    @pl.when(lo < hi)
    def _():
        def load(level):
            return pltpu.make_async_copy(x_in.at[:, level], x.at[:, level], xsem.at[level])

        begin = jnp.maximum(lo - 2, 0)
        lax.fori_loop(begin, jnp.minimum(hi + 2, LEV), lambda l, _: (load(l).start(), 0)[1], 0)
        lax.fori_loop(begin, jnp.maximum(lo, 1), lambda l, _: (load(l).wait(), 0)[1], 0)

        def ready(level):
            @pl.when(level < LEV - 1)
            def _():
                load(level + 1).wait()

        own_work(x, s1, s2, out_x, rb, cb, sem, ready, lo, hi)


def own(x, early, passed):
    shapes = [v.shape for v in passed] if not early else [v.shape for v in passed] + list(KEPT)
    aliased = {i + 1: i for i in range(len(passed))}
    return pl.pallas_call(
        functools.partial(own_kernel, early, len(shapes) + len(passed) - 3),
        out_shape=tuple(jax.ShapeDtypeStruct(k, F32) for k in shapes),
        in_specs=[ANY] * (1 + len(passed)),
        out_specs=(ANY,) * len(shapes),
        input_output_aliases=aliased,
        scratch_shapes=[STATE, STATE, STATE, pltpu.SemaphoreType.DMA, pltpu.SemaphoreType.DMA((LEV,))],
        compiler_params=pltpu.CompilerParams(vmem_limit_bytes=VMEM_ALL),
        name="own_early" if early else "own_late",
    )(x, *passed)


def row_terms(near, far, mid, edge, kept, sign):
    lane, sub = lanes(), sublanes()
    zero = jnp.zeros((8, 128), F32)

    def at(ref, f, st, lt):
        return ref[f * 16 + st * 8 : f * 16 + st * 8 + 8, lt * 128 : lt * 128 + 128]

    def full(src, out, put):
        for lt in range(8):
            for st in range(2):
                c, left, right, four = {}, {}, {}, {}
                o = [at(out, f, st, lt) for f in range(3)]
                for f in range(3):
                    c[f] = at(src, f, st, lt)
                    lo = pltpu.roll(at(src, f, st, lt - 1), 1, 1) if lt > 0 else zero
                    hi = pltpu.roll(at(src, f, st, lt + 1), 127, 1) if lt < 7 else zero
                    left[f] = jnp.where(lane == 0, lo, pltpu.roll(c[f], 1, 1))
                    right[f] = jnp.where(lane == 127, hi, pltpu.roll(c[f], 127, 1))
                    other = at(src, f, 1 - st, lt)
                    above = jnp.where(sub == 0, c[f] if st == 0 else pltpu.roll(other, 1, 0), pltpu.roll(c[f], 1, 0))
                    below = jnp.where(sub == 7, c[f] if st == 1 else pltpu.roll(other, 7, 0), pltpu.roll(c[f], 7, 0))
                    four[f] = 2.0 * (left[f] + right[f] + o[f]) + (above + below)
                e = 0.06 * c[1] + 0.1 * (four[0] + (left[2] - right[2]))
                n = 0.1 * (four[1] + sign * o[2]) - 0.06 * c[0]
                h = 0.1 * (four[2] + (left[0] - right[0]) + sign * o[1])
                put(st, lt, (e, n, h))

    def put_edge(st, lt, new):
        for f in range(3):
            edge[f * 16 + st * 8 : f * 16 + st * 8 + 8, lt * 128 : lt * 128 + 128] = new[f]

    full(near, far, put_edge)
    for lt in range(8):
        for st in range(2):
            y = upright([at(near, f, st, lt) for f in range(3)], sign)
            z = upright(y, sign)
            for f in range(3):
                rows, cols = slice(f * 16 + st * 8, f * 16 + st * 8 + 8), slice(lt * 128, lt * 128 + 128)
                mid[rows, cols] = y[f]
                kept[48 + f * 16 + st * 8 : 48 + f * 16 + st * 8 + 8, cols] += z[f]

    def put_kept(st, lt, new):
        for f in range(3):
            kept[f * 16 + st * 8 : f * 16 + st * 8 + 8, lt * 128 : lt * 128 + 128] += new[f]

    full(mid, edge, put_kept)


def column_terms(tiles, comp):
    lane, sub = lanes(), sublanes()
    flip = jnp.where(comp == 1, 1.0, -1.0)
    right_half = comp == 1
    x1, x2 = [[], [], []], [[], [], []]
    for v in tiles:
        w = pltpu.roll(v, 127, 1)
        a = jnp.where(right_half, w, v)
        b = jnp.where(right_half, v, w)
        for f in range(3):
            x1[f].append(pltpu.roll(a, (128 - 32 * f) % 128, 1))
            x2[f].append(pltpu.roll(b, (128 - 32 * f) % 128, 1))

    def lateral(v):
        per_tile = [sideways([v[f][k] for f in range(3)], flip) for k in range(len(v[0]))]
        return [[p[f] for p in per_tile] for f in range(3)]

    def full(c, out):
        res = [[], [], []]
        for rt in range(2):
            prev, nxt, four = {}, {}, {}
            for f in range(3):
                v = c[f][rt]
                p = c[f][2] if rt == 0 else c[f][0]
                q = c[f][1] if rt == 0 else c[f][2]
                prev[f] = jnp.where(sub == 0, pltpu.roll(p, 1, 0), pltpu.roll(v, 1, 0))
                nxt[f] = jnp.where(sub == 7, pltpu.roll(q, 7, 0), pltpu.roll(v, 7, 0))
                above = jnp.where(lane < 2, v, pltpu.roll(v, 2, 1))
                below = jnp.where(lane >= 30, v, pltpu.roll(v, 126, 1))
                four[f] = 2.0 * (prev[f] + nxt[f] + out[f][rt]) + (above + below)
            res[0].append(0.06 * c[1][rt] + 0.1 * (four[0] + flip * out[2][rt]))
            res[1].append(0.1 * (four[1] + (prev[2] - nxt[2])) - 0.06 * c[0][rt])
            res[2].append(0.1 * (four[2] + flip * out[0][rt] + (prev[1] - nxt[1])))
        return res

    y = lateral(x1)
    s0 = full(y, full(x1, x2))
    s1 = lateral([[v[0], v[1]] for v in y])
    pairs = []
    for f in range(3):
        row = []
        for rt in range(2):
            a = jnp.where(right_half, s0[f][rt], s1[f][rt])
            b = jnp.where(right_half, s1[f][rt], s0[f][rt])
            row.append(jnp.where(lane % 2 == 0, a, pltpu.roll(b, 1, 1)))
        pairs.append(row)
    return pairs


def rows_kernel(pay_up, pay_dn, x_own, rb, out_x, ke, halo_rows, mid, edge, kept, sems):
    comp = lax.axis_index("comp")
    loads = [
        pltpu.make_async_copy(rb, kept, sems.at[0]),
        pltpu.make_async_copy(pay_up.at[pl.ds(0, 96), :], halo_rows.at[0], sems.at[0]),
        pltpu.make_async_copy(pay_dn.at[pl.ds(0, 96), :], halo_rows.at[1], sems.at[0]),
    ]
    for c in loads:
        c.start()
    for c in loads:
        c.wait()
    rest = pl.multiple_of(comp * 128, 128)
    es = pl.multiple_of((1 - comp) * (COLS - 128), 128)
    puts = [
        pltpu.make_async_copy(
            kept.at[pl.ds((k * 3 + f) * 16, 16), pl.ds(rest, COLS - 128)],
            out_x.at[f, :, r, pl.ds(rest, COLS - 128)],
            sems.at[1],
        )
        for k, r in enumerate((0, 1, 15, 14))
        for f in range(3)
    ]
    for side, there in enumerate(neighbours()):

        @pl.when(there)
        def _():
            rows = halo_rows.at[side]
            row_terms(
                rows.at[pl.ds(0, 48)], rows.at[pl.ds(48, 48)], mid, edge,
                kept.at[pl.ds(side * 96, 96)], 1.0 if side == 0 else -1.0,
            )

        for c in puts[side * 6 : side * 6 + 6]:
            c.start()
    puts.append(pltpu.make_async_copy(kept.at[:, pl.ds(es, 128)], ke, sems.at[1]))
    puts[-1].start()
    for c in puts:
        c.wait()


def rows(pay_up, pay_dn, x_own, rb):
    sds = jax.ShapeDtypeStruct
    return pl.pallas_call(
        rows_kernel,
        out_shape=(sds(x_own.shape, F32), sds((192, 128), F32)),
        in_specs=[ANY] * 4,
        out_specs=(ANY, ANY),
        input_output_aliases={2: 0},
        scratch_shapes=[
            pltpu.VMEM((2, 96, COLS), F32),
            pltpu.VMEM((48, COLS), F32),
            pltpu.VMEM((48, COLS), F32),
            pltpu.VMEM((192, COLS), F32),
            pltpu.SemaphoreType.DMA((2,)),
        ],
        compiler_params=pltpu.CompilerParams(vmem_limit_bytes=VMEM_ALL),
        name="rows",
    )(pay_up, pay_dn, x_own, rb)


def final_kernel(
    x, ex, air, flow, warm, water, part, tally, wgt, pay_up, pay_dn, swp, x_own, ke, cb,
    out_x, out_flow, out_warm,
    s0, s1, kept, cbv, cbo, coef, blocks, wv, res, oc, mask, of, ow, small, sems,
):
    comp = lax.axis_index("comp")
    tile = lax.axis_index("tile")
    lane, sub = lanes(), sublanes()
    has_above, has_below = neighbours()

    def halo(pay, rows, third):
        out = []
        for d in range(2):
            for f in range(3):
                for lv in range(3 - d):
                    out.append((pay.at[(d * 3 + f) * 16 + lv, :], s0.at[f, lv, rows[d], pl.ds(0, COLS)]))
        for f in range(3):
            out.append((pay.at[104 + f, :], s0.at[f, 0, rows[2], pl.ds(0, COLS)]))
        to = pl.ds(0, OCOLS)
        for k in range(2):
            out.append((pay.at[107 + k, :], coef.at[k, rows[0], :]))
            cols = pl.ds(k * OCOLS, OCOLS)
            out.append((pay.at[pl.ds(96, 8), cols], oc.at[pl.ds(k * 10, 8), third, to]))
            for lv in (8, 9):
                out.append((pay.at[101 + lv, cols], oc.at[k * 10 + lv, third, to]))
        out.append((pay.at[111, to], oc.at[20, third, to]))
        return [pltpu.make_async_copy(a, b, sems.at[1]) for a, b in out]

    above = ((23, 22, 21), 8)
    below = ((16, 17, 18), 15)
    keeps = [pltpu.make_async_copy(ke, kept, sems.at[2]), pltpu.make_async_copy(cb, cbv, sems.at[2])]
    smalls = [pltpu.make_async_copy(swp, small, sems.at[3])]
    mine = [
        pltpu.make_async_copy(x.at[:, pl.ds(0, 3)], s0.at[:, :, pl.ds(0, 16), pl.ds(0, COLS)], sems.at[4]),
        pltpu.make_async_copy(ex, coef.at[0, pl.ds(0, 16), :], sems.at[4]),
        pltpu.make_async_copy(air, coef.at[1, pl.ds(0, 16), :], sems.at[4]),
        pltpu.make_async_copy(flow.at[0], oc.at[pl.ds(0, 10), pl.ds(0, 8), pl.ds(0, OCOLS)], sems.at[4]),
        pltpu.make_async_copy(flow.at[1], oc.at[pl.ds(10, 10), pl.ds(0, 8), pl.ds(0, OCOLS)], sems.at[4]),
        pltpu.make_async_copy(warm, oc.at[20, pl.ds(0, 8), pl.ds(0, OCOLS)], sems.at[4]),
        pltpu.make_async_copy(water, mask, sems.at[4]),
    ]
    wcopy = pltpu.make_async_copy(wgt, wv, sems.at[5])

    halos = halo(pay_up, *above) + halo(pay_dn, *below)
    for c in halos:
        c.start()
    for c in smalls + mine + keeps + [wcopy]:
        c.start()
    for c in smalls:
        c.wait()

    row_ok = jnp.where(sub >= 4, has_above.astype(jnp.int32), has_below.astype(jnp.int32)) > 0
    row_halo = jnp.where(sub < 4, has_above.astype(jnp.int32), has_below.astype(jnp.int32)) > 0
    edge2 = jnp.where(comp == 0, lane, 127 - lane) < 2
    edge1 = jnp.where(comp == 0, lane, 127 - lane) < 1
    corner = jnp.where(row_ok, small[24:32, :], 0.0)
    for f in range(3):
        for lv in range(3):
            shift = (128 - 2 * (f * 16 + lv) + 126 * comp) % 128
            for rt in range(3):
                v = small[rt * 8 : rt * 8 + 8, :] if rt < 2 else corner
                s0[f, lv, rt * 8 : rt * 8 + 8, COLS:WIDE] = jnp.where(edge2, pltpu.roll(v, shift, 1), 0.0)

    for c in mine:
        c.wait()
    for c in halos:
        c.wait()

    @pl.when(jnp.logical_not(has_above & has_below))
    def _():
        for lt in range(8):
            cols = slice(lt * 128, lt * 128 + 128)
            for f in range(3):
                for lv in range(3):
                    s0[f, lv, 16:24, cols] = jnp.where(row_ok, s0[f, lv, 16:24, cols], 0.0)

        def oclear(g, _):
            for lt in range(4):
                cols = slice(lt * 128, lt * 128 + 128)
                oc[g, 8:16, cols] = jnp.where(row_halo, oc[g, 8:16, cols], 0.0)
            return 0

        lax.fori_loop(0, 21, oclear, 0)

    for level in range(2):

        def put_first(rt, lt, new):
            rows, cols = slice(rt * 8, rt * 8 + 8), slice(lt * 128, lt * 128 + 128)
            for f in range(3):
                v = new[f]
                if lt == 8:
                    v = jnp.where(edge1 & row_ok if rt == 2 else edge1, v, 0.0)
                elif rt == 2:
                    v = jnp.where(row_ok, v, 0.0)
                s1[f, level, rows, cols] = v

        sweep(s0, level, 0, level + 1, range(3), range(9), True, None, put_first)

    def put_flux(rt, lt, new):
        rows, cols = slice(rt * 8, rt * 8 + 8), slice(lt * 128, lt * 128 + 128)
        e, n, h = new
        mult = coef[0, rows, cols] * jnp.sqrt(e * e + n * n + 0.25)
        at = rt * 512 + lt * 8
        for f, v in enumerate((mult * e, mult * n, mult * (coef[1, rows, cols] - h))):
            hi = v.astype(jnp.bfloat16).astype(F32)
            blocks[pl.ds(at + f, 8, stride=64), :] = hi
            blocks[pl.ds(at + 3 + f, 8, stride=64), :] = v - hi
        blocks[pl.ds(at + 6, 8, stride=64), :] = jnp.ones((8, 128), F32)
        blocks[pl.ds(at + 7, 8, stride=64), :] = jnp.zeros((8, 128), F32)

    sweep(s1, 0, 0, 1, range(3), range(8), True, None, put_flux)

    for c in keeps:
        c.wait()
    es = pl.multiple_of((1 - comp) * (COLS - 128), 128)
    pairs = column_terms((small[0:8, :], small[8:16, :], corner), comp)
    own2 = jnp.where(comp == 0, 127 - lane, lane) < 2
    for f in range(3):
        for lv in range(16):
            shift = (128 - 2 * lv + 126 * (1 - comp)) % 128
            for rt in range(2):
                v = cbv[f, lv, rt * 8 : rt * 8 + 8, :]
                for k, at in ((0, 0), (1, 1)) if rt == 0 else ((2, 7), (3, 6)):
                    line = kept[(k * 3 + f) * 16 + lv : (k * 3 + f) * 16 + lv + 1, :]
                    v = jnp.where(sub == at, line, v)
                v = v + jnp.where(own2, pltpu.roll(pairs[f][rt], shift, 1), 0.0)
                cbo[f, lv, rt * 8 : rt * 8 + 8, :] = v
    put_edge = pltpu.make_async_copy(cbo, out_x.at[:, :, :, pl.ds(es, 128)], sems.at[7])
    put_edge.start()

    wcopy.wait()
    base = tile * 128

    def remap(g, _):
        live = tally[g]
        parts = []
        for s in range(4):
            p = part[s, g] - base
            p = jnp.where(p < 0, p + 192, p)
            row = pl.multiple_of(p * 8, 8)
            v = blocks[pl.ds(row, 8), :]
            parts.append(v * jnp.where(s < live, 1.0, 0.0))
        lhs = jnp.concatenate(parts, axis=1).astype(jnp.bfloat16)
        rhs = wv[g].reshape(512, 128)
        res[pl.ds(pl.multiple_of(g * 8, 8), 8), :] = jnp.dot(lhs, rhs, preferred_element_type=F32)
        return 0

    lax.fori_loop(0, 32, remap, 0, unroll=4)

    def unpack_ocean():
        for g in range(21):
            shift = (128 - g + 127 * comp) % 128
            v = pltpu.roll(small[16:24, :], shift, 1)
            oc[g, 0:8, OCOLS:OWIDE] = jnp.where(edge1, v, 0.0)

    unpack_ocean()

    def around(g, lt):
        cols = slice(lt * 128, lt * 128 + 128)
        c = oc[g, 0:8, cols]
        hv = oc[g, 8:16, cols]
        lo, hi = (lt - 1) % 5, lt + 1
        left = jnp.where(lane == 0, pltpu.roll(oc[g, 0:8, lo * 128 : lo * 128 + 128], 1, 1), pltpu.roll(c, 1, 1))
        right = jnp.where(lane == 127, pltpu.roll(oc[g, 0:8, hi * 128 : hi * 128 + 128], 127, 1), pltpu.roll(c, 127, 1))
        prev = jnp.where(sub == 0, hv, pltpu.roll(c, 1, 0))
        nxt = jnp.where(sub == 7, hv, pltpu.roll(c, 7, 0))
        return c, left, right, prev, nxt

    for lt in range(4):
        cols = slice(lt * 128, lt * 128 + 128)
        m = mask[:, cols].astype(F32)
        den = res[pl.ds(lt * 8 + 6, 8, stride=32), :]
        rem = [
            (res[pl.ds(lt * 8 + f, 8, stride=32), :] + res[pl.ds(lt * 8 + f + 3, 8, stride=32), :]) / den
            for f in range(3)
        ]
        for k in range(2):
            for lv in range(10):
                g = k * 10 + lv
                c, left, right, prev, nxt = around(g, lt)
                other = oc[(1 - k) * 10 + lv, 0:8, cols]
                vert = oc[k * 10 + max(lv - 1, 0), 0:8, cols] + oc[k * 10 + min(lv + 1, 9), 0:8, cols]
                v = 0.2 * ((left + right) + (prev + nxt)) + 0.1 * vert
                v = v + (0.06 if k == 0 else -0.06) * other
                if lv == 0:
                    v = v + 0.2 * rem[k]
                of[k, lv, :, cols] = m * v
        c, left, right, prev, nxt = around(20, lt)
        lap = (left + right) + (prev + nxt) - 4.0 * c
        carried = oc[0, 0:8, cols] * (0.5 * (right - left)) + oc[10, 0:8, cols] * (0.5 * (nxt - prev))
        ow[:, cols] = c + (m * 0.2) * (rem[2] - carried + 0.5 * lap)
    tail = [
        pltpu.make_async_copy(of, out_flow, sems.at[8]),
        pltpu.make_async_copy(ow, out_warm, sems.at[8]),
    ]
    for c in tail:
        c.start()
    for c in tail + [put_edge]:
        c.wait()


def final(x, ex, air, flow, warm, water, part, tally, wgt, halos, kept):
    sds = jax.ShapeDtypeStruct
    return pl.pallas_call(
        final_kernel,
        out_shape=(sds(x.shape, F32), sds(flow.shape, F32), sds(warm.shape, F32)),
        in_specs=[ANY] * 6 + [SMEM] * 2 + [ANY] * 7,
        out_specs=(ANY, ANY, ANY),
        input_output_aliases={12: 0},
        scratch_shapes=[
            pltpu.VMEM((3, 3, 24, WIDE), F32),
            pltpu.VMEM((3, 2, 24, WIDE), F32),
            pltpu.VMEM((192, 128), F32),
            pltpu.VMEM((3, LEV, ROWS, 128), F32),
            pltpu.VMEM((3, LEV, ROWS, 128), F32),
            pltpu.VMEM((2, 24, COLS), F32),
            pltpu.VMEM((24 * 64, 128), F32),
            pltpu.VMEM((32, 4, 128, 128), jnp.bfloat16),
            pltpu.VMEM((256, 128), F32),
            pltpu.VMEM((21, 16, OWIDE), F32),
            pltpu.VMEM((OROWS, OCOLS), jnp.int32),
            pltpu.VMEM((2, OLEV, OROWS, OCOLS), F32),
            pltpu.VMEM((OROWS, OCOLS), F32),
            pltpu.VMEM((32, 128), F32),
            pltpu.SemaphoreType.DMA((9,)),
        ],
        compiler_params=pltpu.CompilerParams(vmem_limit_bytes=VMEM_ALL),
        name="final",
    )(x, ex, air, flow, warm, water, part, tally, wgt, *halos, *kept)


def shift(v, step, across):
    tiles = lax.axis_size("tile")
    if not across:
        return lax.ppermute(v, "tile", [(t, (t + step) % tiles) for t in range(tiles)])
    perm = [(c * tiles + t, (1 - c) * tiles + (t + step) % tiles) for c in range(2) for t in range(tiles)]
    return lax.ppermute(v, ("comp", "tile"), perm)


def shards(x, ex, air, flow, warm, water, part, tally, wgt):
    pay_up, pay_dn, swp = pack(x, ex, air, flow, warm)
    got_up = shift(pay_up, 1, False)
    pay_dn, *kept = own(x, True, [pay_dn])
    got_dn = shift(pay_dn, -1, False)
    swp, x_own, rb, cb = own(x, False, [swp, *kept])
    upper = lax.broadcasted_iota(jnp.int32, (8, 128), 0) >= 4
    corner = jnp.where(upper, got_up[112:120, :128], got_dn[112:120, :128])
    got_sw = shift(jnp.concatenate([swp, corner], axis=0), 0, True)
    x_own, ke = rows(got_up, got_dn, x_own, rb)
    return final(x, ex, air, flow, warm, water, part.T, tally, wgt, (got_up, got_dn, got_sw), (x_own, ke, cb))


def solution(mesh):
    placed = (
        P(None, None, "tile", "comp"),
        P("tile", "comp"),
        P("tile", "comp"),
        P(None, None, "tile", "comp"),
        P("tile", "comp"),
        P("tile", "comp"),
        P(("comp", "tile"), None),
        P(("comp", "tile")),
        P(("comp", "tile"), None, None, None),
    )
    return jax.shard_map(
        shards,
        mesh=mesh,
        in_specs=placed,
        out_specs=(P(None, None, "tile", "comp"), P(None, None, "tile", "comp"), P("tile", "comp")),
        check_vma=False,
    )
```

time: 46 us -> 36.2 us (0.79)
  the two profiles are of different devices: /device:TPU:8 before, /device:TPU:1 now
where the time goes in v2:
time: 36.2 us; the launch traced here: 35.9 us
  Pallas kernels  24 us (66%)
  starting transfers between devices  9.2 us (25%)
  other arithmetic  1.46 us (4%)
  between operations  0.71 us (2%)
  local copies, waits for them, and re-layouts  0.6 us (2%)
    pallas_call x2, Pallas kernels, own(): pl.pallas_call(functools.partial(own_kernel, early, len(shapes) + len(pas...  10.8 us
    pallas_call x1, Pallas kernels, final(): pl.pallas_call(final_kernel, out_shape=(sds(x.shape, F32), sds(flow.shape...  6.61 us
    ppermute x2, starting transfers between devices, shift(): lax.ppermute(v, 'tile', [(t, (t + step) % tiles) for t in range(tiles)])  6.54 us
    pallas_call x1, Pallas kernels, pack(): pl.pallas_call(pack_kernel, out_shape=(sds((128, COLS), F32), sds((120, C...  3.53 us
    pallas_call x1, Pallas kernels, rows(): pl.pallas_call(rows_kernel, out_shape=(sds(x_own.shape, F32), sds((192, 1...  3.06 us
    ppermute x1, starting transfers between devices, shift(): return lax.ppermute(v, ('comp', 'tile'), perm)  2.66 us
    select_n x1, other arithmetic, shards(): corner = jnp.where(upper, got_up[112:120, :128], got_dn[112:120, :128])  0.75 us
  transfers between devices with their start and end apart: 3, of which 0 were waited for; matrix products, arithmetic and copies ran while one was open for 0% of the time, Pallas kernels for 38%

profile of v2, /device:TPU:1, one launch (start us, length us, event | category | flops | bytes accessed | tf_op | source)
XLA Modules:
  0.0 35.9 jit_solution(18040993847740334000)
XLA Ops:
  0.6 3.5 %pack.1 = (f32[128,1024]{1,0:T(8,128)}, f32[120,1024]{1,0:T(8,128)}, f32[24,128]{1,0:T(8,128)}) custom-call(f32[3,16,16,1024]{3,2,1,0:T(8,128)} %x.1, f32[16,1024]{1,0:T(8,128)} %ex.1, f32[16,1024]{1,0:T(8,128)} %air.1, f32[2,10,8,512]{3,2,1,0:T(8,128)} %flow.1, f32[8,512]{1,0:T(8,128)} %warm.1), custom_call_target="tpu_custom_call" | custom-call | tf_op jit(solution)/shard_map/pack/pallas_call | solution.py:253
  4.2 3.1 %collective-permute-start = (f32[128,1024]{1,0:T(8,128)}, f32[128,1024]{1,0:T(8,128)S(1)}, u32[]{:S(2)}, u32[]{:S(2)}) collective-permute-start(f32[128,1024]{1,0:T(8,128)} %get-tuple-element.16), channel_id=1, source_target_pairs={{0,1},{1,2},{2,3},{3,4},{4,5},{5,6},{6,7},{7,8},{8,9},{9,10},{10,1... | collective-permute-start | bytes 1572872 | tf_op jit(solution)/shard_map/ppermute | solution.py:704
  7.3 5.3 %own_early.1 = (f32[120,1024]{1,0:T(8,128)}, f32[3,16,16,1024]{3,2,1,0:T(8,128)}, f32[192,1024]{1,0:T(8,128)}, f32[3,16,16,128]{3,2,1,0:T(8,128)}) custom-call(f32[3,16,16,1024]{3,2,1,0:T(8,128)} %x.1, f32[120,1024]{1,0:T(8,128)} %get-tuple-element.17.refs_0_), custom_call_target="tpu_custom_call", output_to_operand_aliasing={{0}: (1, {})} | custom-call | tf_op jit(solution)/shard_map/own_early/pallas_call | solution.py:301
  12.6 3.4 %collective-permute-start.1 = (f32[120,1024]{1,0:T(8,128)}, f32[120,1024]{1,0:T(8,128)}, u32[]{:S(2)}, u32[]{:S(2)}) collective-permute-start(f32[120,1024]{1,0:T(8,128)} %get-tuple-element.18), channel_id=1, source_target_pairs={{0,127},{1,0},{2,1},{3,2},{4,3},{5,4},{6,5},{7,6},{8,7},{9,8},{10,... | collective-permute-start | bytes 1474568 | tf_op jit(solution)/shard_map/ppermute | solution.py:704
  16.1 5.4 %own_late.1 = (f32[24,128]{1,0:T(8,128)}, f32[3,16,16,1024]{3,2,1,0:T(8,128)}, f32[192,1024]{1,0:T(8,128)}, f32[3,16,16,128]{3,2,1,0:T(8,128)}) custom-call(f32[3,16,16,1024]{3,2,1,0:T(8,128)} %x.1, f32[24,128]{1,0:T(8,128)} %get-tuple-element.19.refs_0_, ...), custom_call_target="tpu_custom_call", output_to_operand_aliasing={{0}: (1, {}), {1}: (2, {}), {2}: (3, {}), {3}: (4, {})} | custom-call | tf_op jit(solution)/shard_map/own_late/pallas_call | solution.py:301
  21.5 0.0 collective-permute-done.1.pay_dn
  21.5 0.0 collective-permute-done.pay_up
  21.5 0.0 copy-start
  21.5 0.7 %slice_select_fusion = f32[8,128]{1,0:T(8,128)S(1)} fusion(f32[120,1024]{1,0:T(8,128)} %collective-permute-done.1.pay_dn, f32[128,1024]{1,0:T(8,128)S(1)} %collective-permute-done.pay_up, pred[8]{0:T(512)(128)(4,1)S(1)} %iota_compare_fusion), kind=kLoop, calls=%fused_computation.1 | loop fusion | flops 1024 | bytes 12296 | tf_op jit(solution)/shard_map/jit(_where)/select_n | solution.py:716
  22.3 0.7 %pad_maximum_fusion = f32[32,128]{1,0:T(8,128)S(1)} fusion(f32[8,128]{1,0:T(8,128)S(1)} %slice_select_fusion, f32[24,128]{1,0:T(8,128)} %get-tuple-element.23), kind=kLoop, calls=%fused_computation | loop fusion | flops 4096 | bytes 32768 | tf_op jit(solution)/shard_map/concatenate | solution.py:717
  23.0 2.7 %collective-permute-start.2 = (f32[32,128]{1,0:T(8,128)S(1)}, f32[32,128]{1,0:T(8,128)S(1)}, u32[]{:S(2)}, u32[]{:S(2)}) collective-permute-start(f32[32,128]{1,0:T(8,128)S(1)} %pad_maximum_fusion), channel_id=1, source_target_pairs={{0,128},{1,129},{2,130},{3,131},{4,132},{5,133},{6,134},{7,135},{8... | collective-permute-start | bytes 49160 | tf_op jit(solution)/shard_map/ppermute | solution.py:706
  25.6 0.0 copy-done
  25.6 3.1 %rows.1 = (f32[3,16,16,1024]{3,2,1,0:T(8,128)}, f32[192,128]{1,0:T(8,128)}) custom-call(f32[128,1024]{1,0:T(8,128)} %copy-done, f32[120,1024]{1,0:T(8,128)} %collective-permute-done.1.pay_dn, f32[3,16,16,1024]{3,2,1,0:T(8,128)} %get-tuple-element.24.x_own, f32[192,1024]{1,0:T(8,128)} %get-tuple-element.25.rb), custom_call_target="tpu_custom_call", output_to_operand_aliasing={{0}: (2, {})} | custom-call | tf_op jit(solution)/shard_map/rows/pallas_call | solution.py:452
  28.7 0.0 collective-permute-done.2.swp
  28.7 0.0 copy-start.1
  28.7 0.6 %copy-done.1 = f32[32,128]{1,0:T(8,128)} copy-done((f32[32,128]{1,0:T(8,128)}, f32[32,128]{1,0:T(8,128)S(1)}, u32[]{:S(2)}) %copy-start.1) | copy-done | bytes 16408
  29.3 6.6 %final.1 = (f32[3,16,16,1024]{3,2,1,0:T(8,128)}, f32[2,10,8,512]{3,2,1,0:T(8,128)}, f32[8,512]{1,0:T(8,128)}) custom-call(f32[3,16,16,1024]{3,2,1,0:T(8,128)} %x.1, f32[16,1024]{1,0:T(8,128)} %ex.1, f32[16,1024]{1,0:T(8,128)} %air.1, f32[2,10,8,512]{3,2,1,0:T(8,128)} %flow.1, f32[8,512]{1,0:T(8,128)} %warm.1, ...), custom_call_target="tpu_custom_call", output_to_operand_aliasing={{0}: (12, {})} | custom-call | tf_op jit(solution)/shard_map/final/pallas_call | solution.py:673
  (1 shorter events, 0.0 us)
Async XLA Ops:
  4.2 17.3 %collective-permute-start = (f32[128,1024]{1,0:T(8,128)}, f32[128,1024]{1,0:T(8,128)S(1)}, u32[]{:S(2)}, u32[]{:S(2)}) collective-permute-start(f32[128,1024]{1,0:T(8,128)} %get-tuple-element.16), channel_id=1, source_target_pairs={{0,1},{1,2},{2,3},{3,4},{4,5},{5,6},{6,7},{7,8},{8,9},{9,10},{10,1... | collective-permute-start | bytes 1572872 | tf_op jit(solution)/shard_map/ppermute | solution.py:704
  12.6 8.9 %collective-permute-start.1 = (f32[120,1024]{1,0:T(8,128)}, f32[120,1024]{1,0:T(8,128)}, u32[]{:S(2)}, u32[]{:S(2)}) collective-permute-start(f32[120,1024]{1,0:T(8,128)} %get-tuple-element.18), channel_id=1, source_target_pairs={{0,127},{1,0},{2,1},{3,2},{4,3},{5,4},{6,5},{7,6},{8,7},{9,8},{10,... | collective-permute-start | bytes 1474568 | tf_op jit(solution)/shard_map/ppermute | solution.py:704
  21.5 4.1 %copy-start = (f32[128,1024]{1,0:T(8,128)}, f32[128,1024]{1,0:T(8,128)S(1)}, u32[]{:S(2)}) copy-start(f32[128,1024]{1,0:T(8,128)S(1)} %collective-permute-done.pay_up) | copy-start | bytes 1572868
  23.0 5.7 %collective-permute-start.2 = (f32[32,128]{1,0:T(8,128)S(1)}, f32[32,128]{1,0:T(8,128)S(1)}, u32[]{:S(2)}, u32[]{:S(2)}) collective-permute-start(f32[32,128]{1,0:T(8,128)S(1)} %pad_maximum_fusion), channel_id=1, source_target_pairs={{0,128},{1,129},{2,130},{3,131},{4,132},{5,133},{6,134},{7,135},{8... | collective-permute-start | bytes 49160 | tf_op jit(solution)/shard_map/ppermute | solution.py:706
  28.7 0.6 %copy-start.1 = (f32[32,128]{1,0:T(8,128)}, f32[32,128]{1,0:T(8,128)S(1)}, u32[]{:S(2)}) copy-start(f32[32,128]{1,0:T(8,128)S(1)} %collective-permute-done.2.swp) | copy-start | bytes 49156

commit v3 on v2

--- a/solution.py
+++ b/solution.py
@@ -100,7 +100,7 @@
 
 def share(early):
     place = lax.axis_index("tile") % 16
-    cut = jnp.where(place == 0, LEV, jnp.where(place == 1, LEV // 2, 0))
+    cut = jnp.where(place == 0, LEV // 2, 0)
     return (0, cut) if early else (cut, LEV)
 
 
@@ -183,63 +183,73 @@
     comp = lax.axis_index("comp")
     cs = pl.multiple_of((1 - comp) * (COLS - 128), 128)
     os_ = pl.multiple_of((1 - comp) * (OCOLS - 128), 128)
+    halves = [
+        pltpu.make_async_copy(x_in.at[:, :, pl.ds(rt * 8, 8)], x.at[:, :, pl.ds(rt * 8, 8)], sems.at[2 + rt])
+        for rt in range(2)
+    ]
     loads = [
         pltpu.make_async_copy(a, b, sems.at[1])
-        for a, b in ((x_in, x), (ex_in, ex), (air_in, air), (flow_in, flow), (warm_in, warm))
+        for a, b in ((ex_in, ex), (air_in, air), (flow_in, flow), (warm_in, warm))
     ]
-    for c in loads:
+    for c in halves[::-1] + loads:
         c.start()
 
-    def rows_to(pay, rows, edge, oedge, sem):
+    def rows_to(pay, rows):
         out = []
         for d in range(2):
             for f in range(3):
                 out.append((x.at[f, :, rows[d], :], pay.at[pl.ds((d * 3 + f) * 16, 16), :]))
         for f in range(3):
             out.append((x.at[f, 0, rows[2], :], pay.at[104 + f, :]))
-        out.append((ex.at[edge, :], pay.at[107, :]))
-        out.append((air.at[edge, :], pay.at[108, :]))
+        return [pltpu.make_async_copy(a, b, sems.at[0]) for a, b in out]
+
+    def surface_to(pay, edge, oedge):
+        out = [(ex.at[edge, :], pay.at[107, :]), (air.at[edge, :], pay.at[108, :])]
         for k in range(2):
             cols = pl.ds(k * OCOLS, OCOLS)
             out.append((flow.at[k, pl.ds(0, 8), oedge, :], pay.at[pl.ds(96, 8), cols]))
             for lv in (8, 9):
                 out.append((flow.at[k, lv, oedge, :], pay.at[101 + lv, cols]))
         out.append((warm.at[oedge, :], pay.at[111, pl.ds(0, OCOLS)]))
-        return [pltpu.make_async_copy(a, b, sem) for a, b in out]
-
-    top = ((0, 1, 2), 0, 0)
-    bottom = ((15, 14, 13), 15, 7)
-
-    for c in loads:
-        c.wait()
-
-    sends = rows_to(pay_up, *bottom, sems.at[0]) + rows_to(pay_dn, *top, sems.at[0])
-    for c in sends:
-        c.start()
+        return [pltpu.make_async_copy(a, b, sems.at[0]) for a, b in out]
 
     lane = lanes()
     back = 1 - comp
-    for rt in range(2):
+    sends = []
+
+    def send(some):
+        for c in some:
+            c.start()
+        sends.extend(some)
+
+    for rt, pay, edges in ((1, pay_up, (15, 14, 13)), (0, pay_dn, (0, 1, 2))):
+        halves[rt].wait()
+        send(rows_to(pay, edges))
         acc = jnp.zeros((8, 128), F32)
         for g in range(48):
             v = x[g // 16, g % 16, rt * 8 : rt * 8 + 8, pl.ds(cs, 128)]
             v = pltpu.roll(v, (2 * g + 2 * back) % 128, 1)
             acc = jnp.where(lane // 2 == g, v, acc)
         packed[rt * 8 : rt * 8 + 8, :] = acc
+        send(
+            [
+                pltpu.make_async_copy(
+                    packed.at[pl.ds(rt * 8, 8), :], pay.at[pl.ds(112, 8), pl.ds(0, 128)], sems.at[0]
+                )
+            ]
+        )
+    for c in loads:
+        c.wait()
+    send(surface_to(pay_up, 15, 7) + surface_to(pay_dn, 0, 0))
     acc = jnp.zeros((8, 128), F32)
     for g in range(21):
         v = flow[g // 10, g % 10, :, pl.ds(os_, 128)] if g < 20 else warm[:, pl.ds(os_, 128)]
         v = pltpu.roll(v, g + back, 1)
         acc = jnp.where(lane == g, v, acc)
     packed[16:24, :] = acc
-    swp[...] = packed[...]
-    corners = [
-        pltpu.make_async_copy(packed.at[pl.ds(8, 8), :], pay_up.at[pl.ds(112, 8), pl.ds(0, 128)], sems.at[0]),
-        pltpu.make_async_copy(packed.at[pl.ds(0, 8), :], pay_dn.at[pl.ds(112, 8), pl.ds(0, 128)], sems.at[0]),
-    ]
-    for c in corners:
-        c.start()
-    for c in sends + corners:
+    swp[0:24, :] = packed[...]
+    swp[24:32, :] = jnp.zeros((8, 128), F32)
+    for c in sends:
         c.wait()
 
 
@@ -255,7 +265,7 @@
         out_shape=(
             sds((128, COLS), F32),
             sds((120, COLS), F32),
-            sds((24, 128), F32),
+            sds((32, 128), F32),
         ),
         in_specs=[ANY] * 5,
         out_specs=(ANY, ANY, vm),
@@ -266,7 +276,7 @@
             pltpu.VMEM((2, OLEV, OROWS, OCOLS), F32),
             pltpu.VMEM((OROWS, OCOLS), F32),
             pltpu.VMEM((24, 128), F32),
-            pltpu.SemaphoreType.DMA((2,)),
+            pltpu.SemaphoreType.DMA((4,)),
         ],
         compiler_params=pltpu.CompilerParams(vmem_limit_bytes=VMEM_ALL),
         name="pack",
@@ -614,7 +624,7 @@
         res[pl.ds(pl.multiple_of(g * 8, 8), 8), :] = jnp.dot(lhs, rhs, preferred_element_type=F32)
         return 0
 
-    lax.fori_loop(0, 32, remap, 0, unroll=4)
+    lax.fori_loop(0, 32, remap, 0, unroll=32)
 
     def unpack_ocean():
         for g in range(21):
@@ -714,7 +724,7 @@
     swp, x_own, rb, cb = own(x, False, [swp, *kept])
     upper = lax.broadcasted_iota(jnp.int32, (8, 128), 0) >= 4
     corner = jnp.where(upper, got_up[112:120, :128], got_dn[112:120, :128])
-    got_sw = shift(jnp.concatenate([swp, corner], axis=0), 0, True)
+    got_sw = shift(lax.dynamic_update_slice(swp, corner, (24, 0)), 0, True)
     x_own, ke = rows(got_up, got_dn, x_own, rb)
     return final(x, ex, air, flow, warm, water, part.T, tally, wgt, (got_up, got_dn, got_sw), (x_own, ke, cb))
 

time: 36.2 us -> 33.2 us (0.917)
  Pallas kernels: 24 us -> 20.5 us
  starting transfers between devices: 9.2 us -> 9.79 us
    pallas_call x2, Pallas kernels: 10.8 us -> 8.6 us  [own(): pl.pallas_call(functools.partial(own_kernel, early, len(shapes) + len(pas...]
    ppermute x2, starting transfers between devices: 6.54 us -> 8.61 us  [shift(): lax.ppermute(v, 'tile', [(t, (t + step) % tiles) for t in range(tiles)])]
    ppermute x1, starting transfers between devices: 2.66 us -> 1.18 us  [shift(): return lax.ppermute(v, ('comp', 'tile'), perm)]
    dynamic_update_slice x0 -> x1, other arithmetic: none -> 1.34 us  [shards(): got_sw = shift(lax.dynamic_update_slice(swp, corner, (24, 0)), 0, True)]
    pallas_call x1, Pallas kernels: 6.61 us -> 5.49 us  [final(): pl.pallas_call(final_kernel, out_shape=(sds(x.shape, F32), sds(flow.shape...]
    select_n x1 -> x0, other arithmetic: 0.75 us -> none  [shards(): corner = jnp.where(upper, got_up[112:120, :128], got_dn[112:120, :128])]
    concatenate x1 -> x0, other arithmetic: 0.71 us -> none  [shards(): got_sw = shift(jnp.concatenate([swp, corner], axis=0), 0, True)]
  transfers between devices with their start and end apart: 3 -> 3, of which waited for: 0 -> 1; matrix products, arithmetic and copies ran while one was open for 0% -> 0% of each run, Pallas kernels for 38% -> 35%
where the time goes in v3:
time: 33.2 us; the launch traced here: 33 us
  Pallas kernels  20.5 us (62%)
  starting transfers between devices  9.79 us (29%)
  other arithmetic  1.35 us (4%)
  between operations  0.7 us (2%)
  local copies, waits for them, and re-layouts  0.6 us (2%)
    ppermute x2, starting transfers between devices, shift(): lax.ppermute(v, 'tile', [(t, (t + step) % tiles) for t in range(tiles)])  8.61 us
    pallas_call x2, Pallas kernels, own(): pl.pallas_call(functools.partial(own_kernel, early, len(shapes) + len(pas...  8.6 us
    pallas_call x1, Pallas kernels, final(): pl.pallas_call(final_kernel, out_shape=(sds(x.shape, F32), sds(flow.shape...  5.49 us
    pallas_call x1, Pallas kernels, pack(): pl.pallas_call(pack_kernel, out_shape=(sds((128, COLS), F32), sds((120, C...  3.34 us
    pallas_call x1, Pallas kernels, rows(): pl.pallas_call(rows_kernel, out_shape=(sds(x_own.shape, F32), sds((192, 1...  3.06 us
    dynamic_update_slice x1, other arithmetic, shards(): got_sw = shift(lax.dynamic_update_slice(swp, corner, (24, 0)), 0, True)  1.34 us
    ppermute x1, starting transfers between devices, shift(): return lax.ppermute(v, ('comp', 'tile'), perm)  1.18 us
  transfers between devices with their start and end apart: 3, of which 1 were waited for; matrix products, arithmetic and copies ran while one was open for 0% of the time, Pallas kernels for 35%

profile of v3, /device:TPU:1, one launch (start us, length us, event | category | flops | bytes accessed | tf_op | source)
XLA Modules:
  0.0 33.0 jit_solution(5501851768156873994)
XLA Ops:
  0.6 3.3 %pack.1 = (f32[128,1024]{1,0:T(8,128)}, f32[120,1024]{1,0:T(8,128)}, f32[32,128]{1,0:T(8,128)}) custom-call(f32[3,16,16,1024]{3,2,1,0:T(8,128)} %x.1, f32[16,1024]{1,0:T(8,128)} %ex.1, f32[16,1024]{1,0:T(8,128)} %air.1, f32[2,10,8,512]{3,2,1,0:T(8,128)} %flow.1, f32[8,512]{1,0:T(8,128)} %warm.1), custom_call_target="tpu_custom_call" | custom-call | tf_op jit(solution)/shard_map/pack/pallas_call | solution.py:263
  4.0 3.1 %collective-permute-start = (f32[128,1024]{1,0:T(8,128)}, f32[128,1024]{1,0:T(8,128)S(1)}, u32[]{:S(2)}, u32[]{:S(2)}) collective-permute-start(f32[128,1024]{1,0:T(8,128)} %get-tuple-element.16), channel_id=1, source_target_pairs={{0,1},{1,2},{2,3},{3,4},{4,5},{5,6},{6,7},{7,8},{8,9},{9,10},{10,1... | collective-permute-start | bytes 1572872 | tf_op jit(solution)/shard_map/ppermute | solution.py:714
  7.1 0.2 own_early.1
  7.2 5.5 %collective-permute-start.1 = (f32[120,1024]{1,0:T(8,128)}, f32[120,1024]{1,0:T(8,128)}, u32[]{:S(2)}, u32[]{:S(2)}) collective-permute-start(f32[120,1024]{1,0:T(8,128)} %get-tuple-element.18), channel_id=1, source_target_pairs={{0,127},{1,0},{2,1},{3,2},{4,3},{5,4},{6,5},{7,6},{8,7},{9,8},{10,... | collective-permute-start | bytes 1474568 | tf_op jit(solution)/shard_map/ppermute | solution.py:714
  12.7 8.4 %own_late.1 = (f32[32,128]{1,0:T(8,128)}, f32[3,16,16,1024]{3,2,1,0:T(8,128)}, f32[192,1024]{1,0:T(8,128)}, f32[3,16,16,128]{3,2,1,0:T(8,128)}) custom-call(f32[3,16,16,1024]{3,2,1,0:T(8,128)} %x.1, f32[32,128]{1,0:T(8,128)} %get-tuple-element.19.refs_0_, ...), custom_call_target="tpu_custom_call", output_to_operand_aliasing={{0}: (1, {}), {1}: (2, {}), {2}: (3, {}), {3}: (4, {})} | custom-call | tf_op jit(solution)/shard_map/own_late/pallas_call | solution.py:311
  21.2 0.0 collective-permute-done.1.pay_dn
  21.2 0.0 collective-permute-done.pay_up
  21.2 0.0 copy-start
  21.2 1.3 %fusion = f32[32,128]{1,0:T(8,128)} fusion(f32[32,128]{1,0:T(8,128)} %get-tuple-element.23, f32[120,1024]{1,0:T(8,128)} %collective-permute-done.1.pay_dn, f32[128,1024]{1,0:T(8,128)S(1)} %collective-permute-done.pay_up, pred[8]{0:T(512)(128)(4,1)S(1)} %iota_compare_fusion), kind=kLoop, calls=%fused_computation.1 | loop fusion | flops 1024 | bytes 12296 | tf_op jit(solution)/shard_map/dynamic_update_slice | solution.py:727
  22.6 1.2 %collective-permute-start.2 = (f32[32,128]{1,0:T(8,128)}, f32[32,128]{1,0:T(8,128)S(1)}, u32[]{:S(2)}, u32[]{:S(2)}) collective-permute-start(f32[32,128]{1,0:T(8,128)} %fusion), channel_id=1, source_target_pairs={{0,128},{1,129},{2,130},{3,131},{4,132},{5,133},{6,134},{7,135},{8... | collective-permute-start | bytes 49160 | tf_op jit(solution)/shard_map/ppermute | solution.py:716
  23.8 0.0 copy-done
  23.8 3.1 %rows.1 = (f32[3,16,16,1024]{3,2,1,0:T(8,128)}, f32[192,128]{1,0:T(8,128)}) custom-call(f32[128,1024]{1,0:T(8,128)} %copy-done, f32[120,1024]{1,0:T(8,128)} %collective-permute-done.1.pay_dn, f32[3,16,16,1024]{3,2,1,0:T(8,128)} %get-tuple-element.24.x_own, f32[192,1024]{1,0:T(8,128)} %get-tuple-element.25.rb), custom_call_target="tpu_custom_call", output_to_operand_aliasing={{0}: (2, {})} | custom-call | tf_op jit(solution)/shard_map/rows/pallas_call | solution.py:462
  26.8 0.1 collective-permute-done.2.swp
  26.9 0.0 copy-start.1
  26.9 0.6 %copy-done.1 = f32[32,128]{1,0:T(8,128)} copy-done((f32[32,128]{1,0:T(8,128)}, f32[32,128]{1,0:T(8,128)S(1)}, u32[]{:S(2)}) %copy-start.1) | copy-done | bytes 16408
  27.5 5.5 %final.1 = (f32[3,16,16,1024]{3,2,1,0:T(8,128)}, f32[2,10,8,512]{3,2,1,0:T(8,128)}, f32[8,512]{1,0:T(8,128)}) custom-call(f32[3,16,16,1024]{3,2,1,0:T(8,128)} %x.1, f32[16,1024]{1,0:T(8,128)} %ex.1, f32[16,1024]{1,0:T(8,128)} %air.1, f32[2,10,8,512]{3,2,1,0:T(8,128)} %flow.1, f32[8,512]{1,0:T(8,128)} %warm.1, ...), custom_call_target="tpu_custom_call", output_to_operand_aliasing={{0}: (12, {})} | custom-call | tf_op jit(solution)/shard_map/final/pallas_call | solution.py:683
  (1 shorter events, 0.0 us)
Async XLA Ops:
  4.0 17.3 %collective-permute-start = (f32[128,1024]{1,0:T(8,128)}, f32[128,1024]{1,0:T(8,128)S(1)}, u32[]{:S(2)}, u32[]{:S(2)}) collective-permute-start(f32[128,1024]{1,0:T(8,128)} %get-tuple-element.16), channel_id=1, source_target_pairs={{0,1},{1,2},{2,3},{3,4},{4,5},{5,6},{6,7},{7,8},{8,9},{9,10},{10,1... | collective-permute-start | bytes 1572872 | tf_op jit(solution)/shard_map/ppermute | solution.py:714
  7.2 14.0 %collective-permute-start.1 = (f32[120,1024]{1,0:T(8,128)}, f32[120,1024]{1,0:T(8,128)}, u32[]{:S(2)}, u32[]{:S(2)}) collective-permute-start(f32[120,1024]{1,0:T(8,128)} %get-tuple-element.18), channel_id=1, source_target_pairs={{0,127},{1,0},{2,1},{3,2},{4,3},{5,4},{6,5},{7,6},{8,7},{9,8},{10,... | collective-permute-start | bytes 1474568 | tf_op jit(solution)/shard_map/ppermute | solution.py:714
  21.2 2.5 %copy-start = (f32[128,1024]{1,0:T(8,128)}, f32[128,1024]{1,0:T(8,128)S(1)}, u32[]{:S(2)}) copy-start(f32[128,1024]{1,0:T(8,128)S(1)} %collective-permute-done.pay_up) | copy-start | bytes 1572868
  22.6 4.3 %collective-permute-start.2 = (f32[32,128]{1,0:T(8,128)}, f32[32,128]{1,0:T(8,128)S(1)}, u32[]{:S(2)}, u32[]{:S(2)}) collective-permute-start(f32[32,128]{1,0:T(8,128)} %fusion), channel_id=1, source_target_pairs={{0,128},{1,129},{2,130},{3,131},{4,132},{5,133},{6,134},{7,135},{8... | collective-permute-start | bytes 49160 | tf_op jit(solution)/shard_map/ppermute | solution.py:716
  26.9 0.6 %copy-start.1 = (f32[32,128]{1,0:T(8,128)}, f32[32,128]{1,0:T(8,128)S(1)}, u32[]{:S(2)}) copy-start(f32[32,128]{1,0:T(8,128)S(1)} %collective-permute-done.2.swp) | copy-start | bytes 49156

commit v4 on v3

--- a/solution.py
+++ b/solution.py
@@ -146,7 +146,6 @@
         out_copy(level).start()
         return 0
 
-    lax.fori_loop(lo, hi, second, 0)
     es = pl.multiple_of((1 - comp) * (COLS - 128), 128)
 
     def kept(half):
@@ -162,6 +161,7 @@
 
         @pl.when((lo <= half * 8) & (half * 8 < hi))
         def _():
+            lax.fori_loop(half * 8, half * 8 + 8, second, 0, unroll=2)
             for c in kept(half):
                 c.start()
 
@@ -420,14 +420,14 @@
 def rows_kernel(pay_up, pay_dn, x_own, rb, out_x, ke, halo_rows, mid, edge, kept, sems):
     comp = lax.axis_index("comp")
     loads = [
-        pltpu.make_async_copy(rb, kept, sems.at[0]),
-        pltpu.make_async_copy(pay_up.at[pl.ds(0, 96), :], halo_rows.at[0], sems.at[0]),
-        pltpu.make_async_copy(pay_dn.at[pl.ds(0, 96), :], halo_rows.at[1], sems.at[0]),
+        [
+            pltpu.make_async_copy(rb.at[pl.ds(k * 96, 96), :], kept.at[pl.ds(k * 96, 96), :], sems.at[2 * k]),
+            pltpu.make_async_copy(pay.at[pl.ds(0, 96), :], halo_rows.at[k], sems.at[2 * k]),
+        ]
+        for k, pay in enumerate((pay_up, pay_dn))
     ]
-    for c in loads:
+    for c in loads[0] + loads[1]:
         c.start()
-    for c in loads:
-        c.wait()
     rest = pl.multiple_of(comp * 128, 128)
     es = pl.multiple_of((1 - comp) * (COLS - 128), 128)
     puts = [
@@ -440,6 +440,8 @@
         for f in range(3)
     ]
     for side, there in enumerate(neighbours()):
+        for c in loads[side]:
+            c.wait()
 
         @pl.when(there)
         def _():
@@ -470,7 +472,7 @@
             pltpu.VMEM((48, COLS), F32),
             pltpu.VMEM((48, COLS), F32),
             pltpu.VMEM((192, COLS), F32),
-            pltpu.SemaphoreType.DMA((2,)),
+            pltpu.SemaphoreType.DMA((3,)),
         ],
         compiler_params=pltpu.CompilerParams(vmem_limit_bytes=VMEM_ALL),
         name="rows",
@@ -521,9 +523,7 @@
     wcopy = pltpu.make_async_copy(wgt, wv, sems.at[5])
 
     halos = halo(pay_up, *above) + halo(pay_dn, *below)
-    for c in halos:
-        c.start()
-    for c in smalls + mine + keeps + [wcopy]:
+    for c in smalls + mine + halos + keeps + [wcopy]:
         c.start()
     for c in smalls:
         c.wait()

time: 33.2 us -> 32.5 us (0.979)
  Pallas kernels: 20.5 us -> 19.5 us
    pallas_call x2, Pallas kernels: 8.6 us -> 7.98 us  [own(): pl.pallas_call(functools.partial(own_kernel, early, len(shapes) + len(pas...]
  transfers between devices with their start and end apart: 3 -> 3, of which waited for: 1 -> 1; matrix products, arithmetic and copies ran while one was open for 0% -> 0% of each run, Pallas kernels for 35% -> 34%
where the time goes in v4:
time: 32.5 us; the launch traced here: 32 us
  Pallas kernels  19.5 us (60%)
  starting transfers between devices  9.56 us (29%)
  other arithmetic  1.35 us (4%)
  between operations  0.7 us (2%)
  local copies, waits for them, and re-layouts  0.6 us (2%)
    ppermute x2, starting transfers between devices, shift(): lax.ppermute(v, 'tile', [(t, (t + step) % tiles) for t in range(tiles)])  8.38 us
    pallas_call x2, Pallas kernels, own(): pl.pallas_call(functools.partial(own_kernel, early, len(shapes) + len(pas...  7.98 us
    pallas_call x1, Pallas kernels, final(): pl.pallas_call(final_kernel, out_shape=(sds(x.shape, F32), sds(flow.shape...  5.37 us
    pallas_call x1, Pallas kernels, pack(): pl.pallas_call(pack_kernel, out_shape=(sds((128, COLS), F32), sds((120, C...  3.34 us
    pallas_call x1, Pallas kernels, rows(): pl.pallas_call(rows_kernel, out_shape=(sds(x_own.shape, F32), sds((192, 1...  2.84 us
    dynamic_update_slice x1, other arithmetic, shards(): got_sw = shift(lax.dynamic_update_slice(swp, corner, (24, 0)), 0, True)  1.34 us
    ppermute x1, starting transfers between devices, shift(): return lax.ppermute(v, ('comp', 'tile'), perm)  1.18 us
  transfers between devices with their start and end apart: 3, of which 1 were waited for; matrix products, arithmetic and copies ran while one was open for 0% of the time, Pallas kernels for 34%

profile of v4, /device:TPU:1, one launch (start us, length us, event | category | flops | bytes accessed | tf_op | source)
XLA Modules:
  0.0 32.0 jit_solution(7566349749450003715)
XLA Ops:
  0.6 3.3 %pack.1 = (f32[128,1024]{1,0:T(8,128)}, f32[120,1024]{1,0:T(8,128)}, f32[32,128]{1,0:T(8,128)}) custom-call(f32[3,16,16,1024]{3,2,1,0:T(8,128)} %x.1, f32[16,1024]{1,0:T(8,128)} %ex.1, f32[16,1024]{1,0:T(8,128)} %air.1, f32[2,10,8,512]{3,2,1,0:T(8,128)} %flow.1, f32[8,512]{1,0:T(8,128)} %warm.1), custom_call_target="tpu_custom_call" | custom-call | tf_op jit(solution)/shard_map/pack/pallas_call | solution.py:263
  4.0 3.1 %collective-permute-start = (f32[128,1024]{1,0:T(8,128)}, f32[128,1024]{1,0:T(8,128)S(1)}, u32[]{:S(2)}, u32[]{:S(2)}) collective-permute-start(f32[128,1024]{1,0:T(8,128)} %get-tuple-element.16), channel_id=1, source_target_pairs={{0,1},{1,2},{2,3},{3,4},{4,5},{5,6},{6,7},{7,8},{8,9},{9,10},{10,1... | collective-permute-start | bytes 1572872 | tf_op jit(solution)/shard_map/ppermute | solution.py:714
  7.1 0.2 own_early.1
  7.2 5.3 %collective-permute-start.1 = (f32[120,1024]{1,0:T(8,128)}, f32[120,1024]{1,0:T(8,128)}, u32[]{:S(2)}, u32[]{:S(2)}) collective-permute-start(f32[120,1024]{1,0:T(8,128)} %get-tuple-element.18), channel_id=1, source_target_pairs={{0,127},{1,0},{2,1},{3,2},{4,3},{5,4},{6,5},{7,6},{8,7},{9,8},{10,... | collective-permute-start | bytes 1474568 | tf_op jit(solution)/shard_map/ppermute | solution.py:714
  12.5 7.8 %own_late.1 = (f32[32,128]{1,0:T(8,128)}, f32[3,16,16,1024]{3,2,1,0:T(8,128)}, f32[192,1024]{1,0:T(8,128)}, f32[3,16,16,128]{3,2,1,0:T(8,128)}) custom-call(f32[3,16,16,1024]{3,2,1,0:T(8,128)} %x.1, f32[32,128]{1,0:T(8,128)} %get-tuple-element.19.refs_0_, ...), custom_call_target="tpu_custom_call", output_to_operand_aliasing={{0}: (1, {}), {1}: (2, {}), {2}: (3, {}), {3}: (4, {})} | custom-call | tf_op jit(solution)/shard_map/own_late/pallas_call | solution.py:311
  20.4 0.0 collective-permute-done.1.pay_dn
  20.4 0.0 collective-permute-done.pay_up
  20.4 0.0 copy-start
  20.4 1.3 %fusion = f32[32,128]{1,0:T(8,128)} fusion(f32[32,128]{1,0:T(8,128)} %get-tuple-element.23, f32[120,1024]{1,0:T(8,128)} %collective-permute-done.1.pay_dn, f32[128,1024]{1,0:T(8,128)S(1)} %collective-permute-done.pay_up, pred[8]{0:T(512)(128)(4,1)S(1)} %iota_compare_fusion), kind=kLoop, calls=%fused_computation.1 | loop fusion | flops 1024 | bytes 12296 | tf_op jit(solution)/shard_map/dynamic_update_slice | solution.py:727
  21.7 1.2 %collective-permute-start.2 = (f32[32,128]{1,0:T(8,128)}, f32[32,128]{1,0:T(8,128)S(1)}, u32[]{:S(2)}, u32[]{:S(2)}) collective-permute-start(f32[32,128]{1,0:T(8,128)} %fusion), channel_id=1, source_target_pairs={{0,128},{1,129},{2,130},{3,131},{4,132},{5,133},{6,134},{7,135},{8... | collective-permute-start | bytes 49160 | tf_op jit(solution)/shard_map/ppermute | solution.py:716
  22.9 0.0 copy-done
  22.9 2.8 %rows.1 = (f32[3,16,16,1024]{3,2,1,0:T(8,128)}, f32[192,128]{1,0:T(8,128)}) custom-call(f32[128,1024]{1,0:T(8,128)} %copy-done, f32[120,1024]{1,0:T(8,128)} %collective-permute-done.1.pay_dn, f32[3,16,16,1024]{3,2,1,0:T(8,128)} %get-tuple-element.24.x_own, f32[192,1024]{1,0:T(8,128)} %get-tuple-element.25.rb), custom_call_target="tpu_custom_call", output_to_operand_aliasing={{0}: (2, {})} | custom-call | tf_op jit(solution)/shard_map/rows/pallas_call | solution.py:464
  25.8 0.3 collective-permute-done.2.swp
  26.0 0.0 copy-start.1
  26.0 0.6 %copy-done.1 = f32[32,128]{1,0:T(8,128)} copy-done((f32[32,128]{1,0:T(8,128)}, f32[32,128]{1,0:T(8,128)S(1)}, u32[]{:S(2)}) %copy-start.1) | copy-done | bytes 16408
  26.6 5.4 %final.1 = (f32[3,16,16,1024]{3,2,1,0:T(8,128)}, f32[2,10,8,512]{3,2,1,0:T(8,128)}, f32[8,512]{1,0:T(8,128)}) custom-call(f32[3,16,16,1024]{3,2,1,0:T(8,128)} %x.1, f32[16,1024]{1,0:T(8,128)} %ex.1, f32[16,1024]{1,0:T(8,128)} %air.1, f32[2,10,8,512]{3,2,1,0:T(8,128)} %flow.1, f32[8,512]{1,0:T(8,128)} %warm.1, ...), custom_call_target="tpu_custom_call", output_to_operand_aliasing={{0}: (12, {})} | custom-call | tf_op jit(solution)/shard_map/final/pallas_call | solution.py:683
  (1 shorter events, 0.0 us)
Async XLA Ops:
  4.0 16.4 %collective-permute-start = (f32[128,1024]{1,0:T(8,128)}, f32[128,1024]{1,0:T(8,128)S(1)}, u32[]{:S(2)}, u32[]{:S(2)}) collective-permute-start(f32[128,1024]{1,0:T(8,128)} %get-tuple-element.16), channel_id=1, source_target_pairs={{0,1},{1,2},{2,3},{3,4},{4,5},{5,6},{6,7},{7,8},{8,9},{9,10},{10,1... | collective-permute-start | bytes 1572872 | tf_op jit(solution)/shard_map/ppermute | solution.py:714
  7.2 13.1 %collective-permute-start.1 = (f32[120,1024]{1,0:T(8,128)}, f32[120,1024]{1,0:T(8,128)}, u32[]{:S(2)}, u32[]{:S(2)}) collective-permute-start(f32[120,1024]{1,0:T(8,128)} %get-tuple-element.18), channel_id=1, source_target_pairs={{0,127},{1,0},{2,1},{3,2},{4,3},{5,4},{6,5},{7,6},{8,7},{9,8},{10,... | collective-permute-start | bytes 1474568 | tf_op jit(solution)/shard_map/ppermute | solution.py:714
  20.4 2.5 %copy-start = (f32[128,1024]{1,0:T(8,128)}, f32[128,1024]{1,0:T(8,128)S(1)}, u32[]{:S(2)}) copy-start(f32[128,1024]{1,0:T(8,128)S(1)} %collective-permute-done.pay_up) | copy-start | bytes 1572868
  21.7 4.3 %collective-permute-start.2 = (f32[32,128]{1,0:T(8,128)}, f32[32,128]{1,0:T(8,128)S(1)}, u32[]{:S(2)}, u32[]{:S(2)}) collective-permute-start(f32[32,128]{1,0:T(8,128)} %fusion), channel_id=1, source_target_pairs={{0,128},{1,129},{2,130},{3,131},{4,132},{5,133},{6,134},{7,135},{8... | collective-permute-start | bytes 49160 | tf_op jit(solution)/shard_map/ppermute | solution.py:716
  26.0 0.6 %copy-start.1 = (f32[32,128]{1,0:T(8,128)}, f32[32,128]{1,0:T(8,128)S(1)}, u32[]{:S(2)}) copy-start(f32[32,128]{1,0:T(8,128)S(1)} %collective-permute-done.2.swp) | copy-start | bytes 49156
